TPU v7x, 32 devices: a whole 2x2x4 slice. The times are simulated.
32 devices in a mesh: section: 4 (over z), head: 8 (over y, x, core).
Axes of the slice: x: 2, y: 2, z: 4, core: 2. Of those that a mesh axis runs over, the one named last changes fastest.
Arguments:
- section_inputs: bfloat16 [4, 256, 1024], P('section'), may hold values from -6 to 6
- section_cotangents: bfloat16 [4, 256, 1024], P('section'), may hold values from -6 to 6
- fresh_tokens: bfloat16 [2, 256, 1024], replicated, may hold values from -6 to 6
- fresh_cotangents: bfloat16 [2, 256, 1024], replicated, may hold values from -6 to 6
- norm_gain: float32 [4, 1024], P('section'), may hold values from 0.1 to 1.9
- query_weight: bfloat16 [4, 1024, 16384], P('section', None, 'head'), as said below
- key_weight: bfloat16 [4, 1024, 16384], P('section', None, 'head'), may hold values from -0.1875 to 0.1875
- value_weight: bfloat16 [4, 1024, 16384], P('section', None, 'head'), may hold values from -0.1875 to 0.1875
- out_weight: bfloat16 [4, 16384, 1024], P('section', 'head'), may hold values from -0.1875 to 0.1875
- saved_inputs: bfloat16 [4, 4, 256, 1024], P('section', None, None, 'head'), may hold values from -6 to 6
- reload_slot: int32 [2, 4], replicated, may hold values from 0 to 3
Outputs:
- next_inputs: bfloat16 [4, 256, 1024], P('section')
- next_cotangents: bfloat16 [4, 256, 1024], P('section')
- saved_after: bfloat16 [4, 4, 256, 1024], P('section', None, None, 'head')
- query_grad: bfloat16 [4, 1024, 16384], P('section', None, 'head')
- key_grad: bfloat16 [4, 1024, 16384], P('section', None, 'head')
- value_grad: bfloat16 [4, 1024, 16384], P('section', None, 'head')
- out_grad: bfloat16 [4, 16384, 1024], P('section', 'head')
- gain_grad: float32 [4, 1024], P('section', 'head')
Inputs may be any that keep to these rules, and one draw needn't show every extreme that they name: `query_weight`: independent entries.
All inputs are finite; a program needn't handle non-finite values.
Results may differ from a plain program's by a relative error of at most 0.015.
The roundings to bfloat16 on the way count: a program that leaves them out, or rounds other values in their place, can miss the bound.
Values may be sent and summed in bfloat16 or wider, within the bound.
A program may use at most 128 MiB of HBM per device.

v0:
```python
import jax
import jax.numpy as jnp
from jax import lax
from jax.sharding import PartitionSpec as P

DK = 128
TICKS = 2


epsilon = 1e-06


def passed_along(value, axis, by):
    count = lax.axis_size(axis)
    pairs = [(i, i + by) for i in range(count) if 0 <= i + by < count]
    return lax.ppermute(value, axis, pairs)


def swapped(value, axis, distance):
    mask = 2**distance
    pairs = [(source, source ^ mask) for source in range(lax.axis_size(axis))]
    return lax.ppermute(value, axis, pairs)


def normalize(rows, gain_row):
    floats = rows.astype(jnp.float32)
    inverse = lax.rsqrt(jnp.mean(floats * floats, axis=-1, keepdims=True) + epsilon)
    unit_rows = floats * inverse
    return ((unit_rows * gain_row).astype(jnp.bfloat16), unit_rows, inverse)


def split_heads(rows):
    return rows.reshape(rows.shape[0], -1, DK)


def attend(normed, query_part, key_part, value_part):
    queries = jnp.dot(normed, query_part, preferred_element_type=jnp.float32).astype(jnp.bfloat16)
    key_rows = jnp.dot(normed, key_part, preferred_element_type=jnp.float32).astype(jnp.bfloat16)
    value_rows = jnp.dot(normed, value_part, preferred_element_type=jnp.float32).astype(
        jnp.bfloat16
    )
    scores = jnp.einsum(
        "qhd,khd->hqk",
        split_heads(queries),
        split_heads(key_rows),
        preferred_element_type=jnp.float32,
    ) * DK ** (-0.5)
    highest = jnp.max(scores, axis=-1, keepdims=True)
    exponent = jnp.exp(scores - highest)
    softmax_rows = exponent / jnp.sum(exponent, axis=-1, keepdims=True)
    softmax_low = softmax_rows.astype(jnp.bfloat16)
    context = jnp.einsum(
        "hqk,khd->qhd", softmax_low, split_heads(value_rows), preferred_element_type=jnp.float32
    )
    context = context.astype(jnp.bfloat16).reshape(normed.shape[0], -1)
    return (queries, key_rows, value_rows, softmax_rows, softmax_low, context)


def ahead(rows, weights):
    gain_row, query_part, key_part, value_part, out_part = weights
    normed, unit_rows, inverse = normalize(rows, gain_row)
    context = attend(normed, query_part, key_part, value_part)[5]
    partial_value = jnp.dot(context, out_part, preferred_element_type=jnp.float32)
    total = lax.psum(partial_value, "head")
    output_rows = (rows.astype(jnp.float32) + total).astype(jnp.bfloat16)
    moved = passed_along(output_rows, "section", 1)
    return moved


def behind(rows, upstream, weights, column_start, share_width):
    gain_row, query_part, key_part, value_part, out_part = weights
    normed, unit_rows, inverse = normalize(rows, gain_row)
    queries, key_rows, value_rows, softmax_rows, softmax_low, context = attend(
        normed, query_part, key_part, value_part
    )
    token_count = rows.shape[0]
    out_term = jnp.dot(context.T, upstream, preferred_element_type=jnp.float32)
    context_grad = jnp.dot(upstream, out_part.T, preferred_element_type=jnp.float32).astype(
        jnp.bfloat16
    )
    softmax_grad = jnp.einsum(
        "qhd,khd->hqk",
        split_heads(context_grad),
        split_heads(value_rows),
        preferred_element_type=jnp.float32,
    )
    value_rows_grad = jnp.einsum(
        "hqk,qhd->khd", softmax_low, split_heads(context_grad), preferred_element_type=jnp.float32
    )
    value_rows_grad = value_rows_grad.astype(jnp.bfloat16).reshape(token_count, -1)
    inner = jnp.sum(softmax_rows * softmax_grad, axis=-1, keepdims=True)
    score_grad = (softmax_rows * (softmax_grad - inner) * DK ** (-0.5)).astype(jnp.bfloat16)
    queries_grad = jnp.einsum(
        "hqk,khd->qhd", score_grad, split_heads(key_rows), preferred_element_type=jnp.float32
    )
    queries_grad = queries_grad.astype(jnp.bfloat16).reshape(token_count, -1)
    key_rows_grad = jnp.einsum(
        "hqk,qhd->khd", score_grad, split_heads(queries), preferred_element_type=jnp.float32
    )
    key_rows_grad = key_rows_grad.astype(jnp.bfloat16).reshape(token_count, -1)
    query_term = jnp.dot(normed.T, queries_grad, preferred_element_type=jnp.float32)
    key_term = jnp.dot(normed.T, key_rows_grad, preferred_element_type=jnp.float32)
    value_term = jnp.dot(normed.T, value_rows_grad, preferred_element_type=jnp.float32)
    normed_part = jnp.dot(queries_grad, query_part.T, preferred_element_type=jnp.float32)
    normed_part = normed_part + jnp.dot(
        key_rows_grad, key_part.T, preferred_element_type=jnp.float32
    )
    normed_part = normed_part + jnp.dot(
        value_rows_grad, value_part.T, preferred_element_type=jnp.float32
    )
    normed_grad = lax.psum(normed_part, "head")
    gain_full = jnp.sum(normed_grad * unit_rows, axis=0)
    unit_grad = normed_grad * gain_row
    along = jnp.mean(unit_grad * unit_rows, axis=-1, keepdims=True)
    returned_rows = (
        upstream.astype(jnp.float32) + inverse * (unit_grad - unit_rows * along)
    ).astype(jnp.bfloat16)
    moved = passed_along(returned_rows, "section", -1)
    gain_term = lax.dynamic_slice_in_dim(gain_full, column_start, share_width, 0)
    return (moved, (query_term, key_term, value_term, out_term, gain_term))


def per_device(
    section_inputs,
    section_cotangents,
    fresh_tokens,
    fresh_cotangents,
    norm_gain,
    query_weight,
    key_weight,
    value_weight,
    out_weight,
    saved_inputs,
    reload_slot,
):
    section_count = lax.axis_size("section")
    section_index = lax.axis_index("section")
    head_index = lax.axis_index("head")
    mirror_index = section_count - 1 - section_index
    share_width = saved_inputs.shape[3]
    column_start = head_index * share_width
    weights = (norm_gain[0], query_weight[0], key_weight[0], value_weight[0], out_weight[0])
    current = section_inputs[0]
    upstream = section_cotangents[0]
    store = saved_inputs[0]
    sums = (
        jnp.zeros(query_weight.shape[1:], jnp.float32),
        jnp.zeros(key_weight.shape[1:], jnp.float32),
        jnp.zeros(value_weight.shape[1:], jnp.float32),
        jnp.zeros(out_weight.shape[1:], jnp.float32),
        jnp.zeros((share_width,), jnp.float32),
    )
    hop_count = section_count.bit_length() - 1
    for tick_number in range(TICKS):
        held_slot = lax.dynamic_index_in_dim(
            reload_slot[tick_number], mirror_index, 0, keepdims=False
        )
        held_block = lax.dynamic_index_in_dim(store, held_slot, 0, keepdims=False)
        own_share = lax.dynamic_slice_in_dim(current, column_start, share_width, 1)
        travel = (own_share, held_block)
        for bit_number in range(hop_count):
            travel = swapped((travel[0], travel[1]), "section", bit_number)
        arrived, reloaded = travel
        store = lax.dynamic_update_index_in_dim(store, arrived, held_slot, 0)
        restored = lax.all_gather(reloaded, "head", axis=1, tiled=True)
        produced = ahead(current, weights)
        returned, terms = behind(restored, upstream, weights, column_start, share_width)
        sums = tuple((total + term for total, term in zip(sums, terms)))
        current = jnp.where(section_index == 0, fresh_tokens[tick_number], produced)
        upstream = jnp.where(
            section_index == section_count - 1, fresh_cotangents[tick_number], returned
        )
    return (
        current[None],
        upstream[None],
        store[None],
        sums[0].astype(jnp.bfloat16)[None],
        sums[1].astype(jnp.bfloat16)[None],
        sums[2].astype(jnp.bfloat16)[None],
        sums[3].astype(jnp.bfloat16)[None],
        sums[4][None],
    )


def solution(mesh):
    placed = (
        P("section", None, None),
        P("section", None, None),
        P(),
        P(),
        P("section", None),
        P("section", None, "head"),
        P("section", None, "head"),
        P("section", None, "head"),
        P("section", "head", None),
        P("section", None, None, "head"),
        P(),
    )
    return jax.shard_map(
        per_device,
        mesh=mesh,
        in_specs=placed,
        out_specs=(
            P("section", None, None),
            P("section", None, None),
            P("section", None, None, "head"),
            P("section", None, "head"),
            P("section", None, "head"),
            P("section", None, "head"),
            P("section", "head", None),
            P("section", "head"),
        ),
        check_vma=False,
    )
```

profile of v0, /device:TPU:0, one launch (start us, length us, event | category | flops | bytes accessed | tf_op | source)
XLA Modules:
  0.0 360.0 jit_solution(5713688471771167253)
XLA Ops:
  9.1 3.1 collective-permute-start.5
  16.9 4.7 %fusion.159 = bf16[32,16,8,128]{3,2,1,0:T(8,128)(2,1)} fusion(bf16[1,1024,2048]{2,1,0:T(8,128)(2,1)} %param.16, bf16[1,256,1024]{2,1,0:T(8,128)(2,1)} %param.11, f32[1024]{0:T(1024)} %bitcast.264, f32[256]{0:T(256)S(1)} %add_rsqrt_fusion.3), kind=kOutput, calls=%fused_computation.124 | convolution fusion | flops 1075314688 | bytes 5772288 | tf_op jit(solution)/shard_map/dot_general | solution.py:37
  21.6 2.3 fusion.153
  28.1 3.1 fusion.266
  35.7 3.1 collective-permute-start.3
  42.7 10.7 %all_gather.6 = bf16[256,1024]{1,0:T(8,128)(2,1)S(1)} all-gather(bf16[256,128]{1,0:T(8,128)(2,1)S(1)} %collective-permute-done.3), channel_id=1, replica_groups=mesh['section'=4,'head'=8] {'head'}, dimensions={1}, use_global_device_ids=true | all-gather | bytes 589824 | tf_op jit(solution)/shard_map/all_gather | solution.py:165
  53.6 4.5 %fusion.78 = bf16[256,2048]{1,0:T(8,128)(2,1)} fusion(bf16[1,1024,2048]{2,1,0:T(8,128)(2,1)} %param.18, bf16[256,1024]{1,0:T(8,128)(2,1)S(1)} %all_gather.6, f32[256]{0:T(256)S(1)} %add_rsqrt_fusion.1, f32[1024]{0:T(1024)S(1)} %bitcast.267), kind=kOutput, calls=%fused_computation.80 | convolution fusion | flops 1075314688 | bytes 5772288 | tf_op jit(solution)/shard_map/dot_general | solution.py:39
  58.1 2.3 fusion.90
  60.4 2.3 fusion.102
  66.5 2.3 copy.63
  68.8 2.8 fusion.270
  71.6 5.1 %fusion.267 = (f32[16,256]{1,0:T(8,128)S(1)}, f32[16,256,256]{1,2,0:T(8,128)}) fusion(bf16[256,16,128]{0,2,1:T(8,128)(2,1)} %bitcast.299, bf16[256,16,128]{0,2,1:T(8,128)(2,1)} %bitcast.297), kind=kOutput, calls=%fused_computation.227 | convolution fusion | flops 271581440 | bytes 6307840 | tf_op jit(solution)/shard_map/sub | solution.py:49
  76.7 4.2 %convolution_convert_fusion.3 = bf16[16,128,256]{2,1,0:T(8,128)(2,1)} fusion(bf16[256,16,128]{0,2,1:T(8,128)(2,1)S(1)} %bitcast.258, f32[16,256,256]{1,2,0:T(8,128)} %get-tuple-element.23, f32[16,256]{1,0:T(8,128)S(1)} %get-tuple-element.22), kind=kOutput, calls=%fused_computation.120 | convolution fusion | flops 271056896 | bytes 6307840 | tf_op jit(solution)/shard_map/hqk,qhd->khd/dot_general | solution.py:87
  81.4 7.6 %fusion.147 = bf16[16,128,256]{2,1,0:T(8,128)(2,1)S(1)} fusion(bf16[256,16,128]{0,2,1:T(8,128)(2,1)} %bitcast.300, f32[16,256,256]{1,2,0:T(8,128)} %fusion.270, f32[16,256,256]{1,2,0:T(8,128)} %get-tuple-element.23, f32[16,256]{1,0:T(8,128)S(1)} %get-tuple-element.22), kind=kOutput, calls=%fused_computation.116 | convolution fusion | flops 276304128 | bytes 10502144 | tf_op jit(solution)/shard_map/hqk,qhd->khd/dot_general | solution.py:97
  89.0 4.5 %fusion.18 = f32[256,1024]{1,0:T(8,128)} fusion(bf16[256,2048]{0,1:T(8,128)(2,1)S(1)} %bitcast.291, bf16[1,1024,2048]{2,1,0:T(8,128)(2,1)} %param.17), kind=kOutput, calls=%fused_computation.22 | convolution fusion | flops 1073741824 | bytes 6291456 | tf_op jit(solution)/shard_map/dot_general | solution.py:105
  93.4 4.7 %fusion.258 = f32[1024,2048]{1,0:T(8,128)} fusion(bf16[256,2048]{0,1:T(8,128)(2,1)S(1)} %bitcast.292, bf16[256,1024]{1,0:T(8,128)(2,1)S(1)} %all_gather.6, f32[256]{0:T(256)S(1)} %add_rsqrt_fusion.1, f32[1024]{0:T(1024)S(1)} %bitcast.270), kind=kOutput, calls=%fused_computation.223 | convolution fusion | flops 1074790400 | bytes 9966592 | tf_op jit(solution)/shard_map/dot_general | solution.py:102
  98.1 8.6 %fusion.144 = bf16[16,128,256]{2,1,0:T(8,128)(2,1)} fusion(bf16[256,16,128]{0,2,1:T(8,128)(2,1)} %bitcast.298, f32[16,256,256]{1,2,0:T(8,128)} %fusion.270, f32[16,256,256]{1,2,0:T(8,128)} %get-tuple-element.23, f32[16,256]{1,0:T(8,128)S(1)} %get-tuple-element.22), kind=kOutput, calls=%fused_computation.115 | convolution fusion | flops 276304128 | bytes 10502144 | tf_op jit(solution)/shard_map/hqk,khd->qhd/dot_general | solution.py:93
  108.1 4.7 %fusion.256 = f32[1024,2048]{1,0:T(8,128)} fusion(bf16[256,2048]{0,1:T(8,128)(2,1)S(1)} %bitcast.287, bf16[256,1024]{1,0:T(8,128)(2,1)S(1)} %all_gather.6, f32[256]{0:T(256)S(1)} %add_rsqrt_fusion.1, f32[1024]{0:T(1024)S(1)} %bitcast.271), kind=kOutput, calls=%fused_computation.222 | convolution fusion | flops 1074790400 | bytes 9966592 | tf_op jit(solution)/shard_map/dot_general | solution.py:103
  112.8 4.7 %fusion.260 = f32[1024,2048]{1,0:T(8,128)} fusion(bf16[256,2048]{0,1:T(8,128)(2,1)S(1)} %bitcast.289, bf16[256,1024]{1,0:T(8,128)(2,1)S(1)} %all_gather.6, f32[256]{0:T(256)S(1)} %add_rsqrt_fusion.1, f32[1024]{0:T(1024)S(1)} %bitcast.272), kind=kOutput, calls=%fused_computation.224 | convolution fusion | flops 1074790400 | bytes 9966592 | tf_op jit(solution)/shard_map/dot_general | solution.py:101
  117.5 4.9 %fusion.223 = f32[2048,1024]{1,0:T(8,128)} fusion(bf16[256,2048]{0,1:T(8,128)(2,1)S(1)} %bitcast.263, bf16[1,256,1024]{2,1,0:T(8,128)(2,1)S(1)} %copy-done.5), kind=kOutput, calls=%fused_computation.184 | convolution fusion | flops 1073741824 | bytes 9961472 | tf_op jit(solution)/shard_map/dot_general | solution.py:77
  123.8 2.4 collective-permute-start.8
  130.2 11.9 %all_gather.7 = bf16[256,1024]{1,0:T(8,128)(2,1)S(1)} all-gather(bf16[256,128]{1,0:T(8,128)(2,1)S(1)} %collective-permute-done.8), channel_id=1, replica_groups=mesh['section'=4,'head'=8] {'head'}, dimensions={1}, use_global_device_ids=true | all-gather | bytes 589824 | tf_op jit(solution)/shard_map/all_gather | solution.py:165
  142.3 4.5 %fusion.81 = bf16[256,2048]{1,0:T(8,128)(2,1)} fusion(bf16[1,1024,2048]{2,1,0:T(8,128)(2,1)} %param.18, bf16[256,1024]{1,0:T(8,128)(2,1)S(1)} %all_gather.7, f32[256]{0:T(256)S(1)} %add_rsqrt_fusion, f32[1024]{0:T(1024)S(1)} %bitcast.273), kind=kOutput, calls=%fused_computation.81 | convolution fusion | flops 1075314688 | bytes 5772288 | tf_op jit(solution)/shard_map/dot_general | solution.py:39
  146.9 2.3 fusion.93
  149.2 2.3 fusion.105
  155.3 2.3 copy.67
  157.5 5.1 %fusion.269 = (f32[16,256]{1,0:T(8,128)S(1)}, f32[16,256,256]{1,2,0:T(8,128)}) fusion(bf16[256,16,128]{0,2,1:T(8,128)(2,1)} %bitcast.293, bf16[256,16,128]{0,2,1:T(8,128)(2,1)} %bitcast.295), kind=kOutput, calls=%fused_computation.229 | convolution fusion | flops 271581440 | bytes 6307840 | tf_op jit(solution)/shard_map/sub | solution.py:49
  162.6 3.8 %convolution_convert_fusion = bf16[16,128,256]{2,1,0:T(8,128)(2,1)} fusion(bf16[256,16,128]{0,2,1:T(8,128)(2,1)S(1)} %bitcast.255, f32[16,256,256]{1,2,0:T(8,128)} %get-tuple-element.27, f32[16,256]{1,0:T(8,128)S(1)} %get-tuple-element.26), kind=kOutput, calls=%fused_computation.117 | convolution fusion | flops 271056896 | bytes 6307840 | tf_op jit(solution)/shard_map/hqk,khd->qhd/dot_general | solution.py:52
  166.4 23.3 %all-reduce.7.cloned.1.call-done = (f32[256,1024]{1,0:T(8,128)}, f32[256,1024]{1,0:T(8,128)}) async-done(((f32[256,1024]{1,0:T(8,128)}, f32[256,1024]{1,0:T(8,128)}), (f32[256,1024]{1,0:T(8,128)}, f32[256,1024]{1,0:T(8,128)})) %all-reduce.7.cloned.1.call-update) | async-done | bytes 2097168 | tf_op jit(solution)/shard_map/psum | solution.py:64
  191.2 3.5 collective-permute-start
  198.5 6.2 %collective-permute-done = bf16[256,1024]{1,0:T(8,128)(2,1)S(1)} collective-permute-done((bf16[256,1024]{1,0:T(8,128)(2,1)S(1)}, bf16[256,1024]{1,0:T(8,128)(2,1)S(1)}, u32[]{:S(2)}, u32[]{:S(2)}) %collective-permute-start) | collective-permute-done | bytes 524320 | tf_op jit(solution)/shard_map/ppermute | solution.py:16
  205.1 2.3 fusion.156
  207.4 2.3 fusion.150
  209.8 2.3 fusion.75
  216.4 2.8 fusion.271
  221.7 8.3 %fusion.141 = bf16[16,128,256]{2,1,0:T(8,128)(2,1)} fusion(bf16[256,16,128]{0,2,1:T(8,128)(2,1)S(1)} %bitcast.294, f32[16,256,256]{1,2,0:T(8,128)} %fusion.271, f32[16,256,256]{1,2,0:T(8,128)} %get-tuple-element.27, f32[16,256]{1,0:T(8,128)S(1)} %get-tuple-element.26), kind=kOutput, calls=%fused_computation.114 | convolution fusion | flops 276304128 | bytes 10502144 | tf_op jit(solution)/shard_map/hqk,qhd->khd/dot_general | solution.py:97
  230.0 8.3 %fusion.138 = bf16[16,128,256]{2,1,0:T(8,128)(2,1)} fusion(bf16[256,16,128]{0,2,1:T(8,128)(2,1)S(1)} %bitcast.296, f32[16,256,256]{1,2,0:T(8,128)} %fusion.271, f32[16,256,256]{1,2,0:T(8,128)} %get-tuple-element.27, f32[16,256]{1,0:T(8,128)S(1)} %get-tuple-element.26), kind=kOutput, calls=%fused_computation.113 | convolution fusion | flops 276304128 | bytes 10502144 | tf_op jit(solution)/shard_map/hqk,khd->qhd/dot_general | solution.py:93
  238.3 2.5 collective-permute-start.10
  243.6 3.3 fusion.268
  249.1 2.3 fusion.10
  258.0 6.9 %fusion.58 = bf16[1,1024,2048]{2,1,0:T(8,128)(2,1)} fusion(f32[1024,2048]{1,0:T(8,128)} %fusion.256, bf16[256,2048]{0,1:T(8,128)(2,1)S(1)} %bitcast.306, bf16[256,1024]{1,0:T(8,128)(2,1)S(1)} %all_gather.7, f32[256]{0:T(256)S(1)} %add_rsqrt_fusion, f32[1024]{0:T(1024)S(1)} %bitcast.281), kind=kOutput, calls=%fused_computation.76 | convolution fusion | flops 1078984704 | bytes 14160896 | tf_op jit(solution)/shard_map/dot_general | solution.py:103
  264.9 6.9 %fusion.56 = bf16[1,1024,2048]{2,1,0:T(8,128)(2,1)} fusion(f32[1024,2048]{1,0:T(8,128)} %fusion.260, bf16[256,2048]{0,1:T(8,128)(2,1)S(1)} %bitcast.308, bf16[256,1024]{1,0:T(8,128)(2,1)S(1)} %all_gather.7, f32[256]{0:T(256)S(1)} %add_rsqrt_fusion, f32[1024]{0:T(1024)S(1)} %bitcast.282), kind=kOutput, calls=%fused_computation.74 | convolution fusion | flops 1078984704 | bytes 14160896 | tf_op jit(solution)/shard_map/dot_general | solution.py:101
  271.8 6.9 %fusion.57 = bf16[1,1024,2048]{2,1,0:T(8,128)(2,1)} fusion(f32[1024,2048]{1,0:T(8,128)} %fusion.258, bf16[256,2048]{0,1:T(8,128)(2,1)S(1)} %bitcast.304, bf16[256,1024]{1,0:T(8,128)(2,1)S(1)} %all_gather.7, f32[256]{0:T(256)S(1)} %add_rsqrt_fusion, f32[1024]{0:T(1024)S(1)} %bitcast.283), kind=kOutput, calls=%fused_computation.75 | convolution fusion | flops 1078984704 | bytes 14160896 | tf_op jit(solution)/shard_map/dot_general | solution.py:102
  278.8 6.7 %fusion.59 = bf16[1,2048,1024]{2,1,0:T(8,128)(2,1)} fusion(f32[2048,1024]{1,0:T(8,128)} %fusion.223, bf16[256,2048]{0,1:T(8,128)(2,1)S(1)} %bitcast.286, bf16[256,1024]{1,0:T(8,128)(2,1)S(1)} %bitcast_select_fusion), kind=kOutput, calls=%fused_computation.77 | convolution fusion | flops 1077936128 | bytes 14155776 | tf_op jit(solution)/shard_map/dot_general | solution.py:77
  285.5 2.5 collective-permute-start.11
  288.0 44.9 %all-reduce.5.cloned.1.call-done = (f32[256,1024]{1,0:T(8,128)}, f32[256,1024]{1,0:T(8,128)}) async-done(((f32[256,1024]{1,0:T(8,128)}, f32[256,1024]{1,0:T(8,128)}), (f32[256,1024]{1,0:T(8,128)}, f32[256,1024]{1,0:T(8,128)})) %all-reduce.5.cloned.1.call-update) | async-done | bytes 2097168 | tf_op jit(solution)/shard_map/psum | solution.py:64
  337.8 4.6 %collective-permute-start.1 = (bf16[256,1024]{1,0:T(8,128)(2,1)S(1)}, bf16[256,1024]{1,0:T(8,128)(2,1)S(1)}, u32[]{:S(2)}, u32[]{:S(2)}) collective-permute-start(bf16[256,1024]{1,0:T(8,128)(2,1)S(1)} %fusion.207), channel_id=1, source_target_pairs={{0,8},{8,16},{16,24},{1,9},{9,17},{17,25},{2,10},{10,18},{18,26},{... | collective-permute-start | bytes 1572872 | tf_op jit(solution)/shard_map/ppermute | solution.py:16
  343.1 7.7 %collective-permute-done.9 = bf16[256,1024]{1,0:T(8,128)(2,1)S(1)} collective-permute-done((bf16[256,1024]{1,0:T(8,128)(2,1)S(1)}, bf16[256,1024]{1,0:T(8,128)(2,1)S(1)}, u32[]{:S(2)}, u32[]{:S(2)}) %collective-permute-start.9) | collective-permute-done | bytes 524320 | tf_op jit(solution)/shard_map/ppermute | solution.py:16
  (159 shorter events, 61.9 us)
Async XLA Ops:
  7.2 14.4 %copy-start.3 = (bf16[1,256,1024]{2,1,0:T(8,128)(2,1)S(1)}, bf16[1,256,1024]{2,1,0:T(8,128)(2,1)}, u32[]{:S(2)}) copy-start(bf16[1,256,1024]{2,1,0:T(8,128)(2,1)} %param.11) | copy-start | bytes 1572868
  7.2 14.4 %copy-start.6 = (f32[1,1024]{1,0:T(1,128)S(1)}, f32[1,1024]{1,0:T(1,128)}, u32[]{:S(2)}) copy-start(f32[1,1024]{1,0:T(1,128)} %param.15) | copy-start | bytes 12292
  7.2 182.5 %all-reduce.7.cloned.1.call-start = ((), (), s32[]{:S(2)}) async-start(), calls=%async_computation.1 | async-start | bytes 4194304 | tf_op jit(solution)/shard_map/psum | solution.py:64
  9.1 33.5 %collective-permute-start.5 = (bf16[256,128]{1,0:T(8,128)(2,1)S(1)}, bf16[256,128]{1,0:T(8,128)(2,1)}, u32[]{:S(2)}, u32[]{:S(2)}) collective-permute-start(bf16[256,128]{1,0:T(8,128)(2,1)S(1)} %dynamic-slice_bitcast_fusion.1), channel_id=1, source_target_pairs={{0,8},{8,0},{16,24},{24,16},{1,9},{9,1},{17,25},{25,17},{2,10},{10... | collective-permute-start | bytes 196616 | tf_op jit(solution)/shard_map/ppermute | solution.py:22
  15.4 6.2 %copy-start.27 = (bf16[1,1024,2048]{2,1,0:T(8,128)(2,1)S(1)}, bf16[1,1024,2048]{2,1,0:T(8,128)(2,1)}, u32[]{:S(2)}) copy-start(bf16[1,1024,2048]{2,1,0:T(8,128)(2,1)} %param.17) | copy-start | bytes 12582916
  15.5 20.2 %collective-permute-start.2 = (bf16[256,128]{1,0:T(8,128)(2,1)S(1)}, bf16[256,128]{1,0:T(8,128)(2,1)}, u32[]{:S(2)}, u32[]{:S(2)}) collective-permute-start(bf16[256,128]{1,0:T(8,128)(2,1)S(1)} %dynamic-slice_bitcast_fusion.2), channel_id=1, source_target_pairs={{0,8},{8,0},{16,24},{24,16},{1,9},{9,1},{17,25},{25,17},{2,10},{10... | collective-permute-start | bytes 196616 | tf_op jit(solution)/shard_map/ppermute | solution.py:22
  31.7 7.1 %copy-start.4 = (bf16[1,256,1024]{2,1,0:T(8,128)(2,1)S(1)}, bf16[1,256,1024]{2,1,0:T(8,128)(2,1)}, u32[]{:S(2)}) copy-start(bf16[1,256,1024]{2,1,0:T(8,128)(2,1)} %param.12) | copy-start | bytes 1572868
  35.7 7.0 %collective-permute-start.3 = (bf16[256,128]{1,0:T(8,128)(2,1)}, bf16[256,128]{1,0:T(8,128)(2,1)S(1)}, u32[]{:S(2)}, u32[]{:S(2)}) collective-permute-start(bf16[256,128]{1,0:T(8,128)(2,1)} %collective-permute-done.2), channel_id=1, source_target_pairs={{0,16},{8,24},{16,0},{24,8},{1,17},{9,25},{17,1},{25,9},{2,18},{10... | collective-permute-start | bytes 196616 | tf_op jit(solution)/shard_map/ppermute | solution.py:22
  42.6 15.5 %copy-start.32 = (bf16[1,1024,2048]{2,1,0:T(8,128)(2,1)S(1)}, bf16[1,1024,2048]{2,1,0:T(8,128)(2,1)}, u32[]{:S(2)}) copy-start(bf16[1,1024,2048]{2,1,0:T(8,128)(2,1)} %param.16) | copy-start | bytes 12582916
  42.6 64.1 %collective-permute-start.6 = (bf16[256,128]{1,0:T(8,128)(2,1)}, bf16[256,128]{1,0:T(8,128)(2,1)S(1)}, u32[]{:S(2)}, u32[]{:S(2)}) collective-permute-start(bf16[256,128]{1,0:T(8,128)(2,1)} %collective-permute-done.5), channel_id=1, source_target_pairs={{0,16},{8,24},{16,0},{24,8},{1,17},{9,25},{17,1},{25,9},{2,18},{10... | collective-permute-start | bytes 196616 | tf_op jit(solution)/shard_map/ppermute | solution.py:22
  76.7 4.2 %copy-start.42 = (f32[16,256,256]{1,2,0:T(8,128)S(1)}, f32[16,256,256]{1,2,0:T(8,128)}, u32[]{:S(2)}) copy-start(f32[16,256,256]{1,2,0:T(8,128)} %get-tuple-element.23) | copy-start | bytes 12582916
  98.1 10.0 %copy-start.8 = (bf16[16,128,256]{2,1,0:T(8,128)(2,1)S(1)}, bf16[16,128,256]{2,1,0:T(8,128)(2,1)}, u32[]{:S(2)}) copy-start(bf16[16,128,256]{2,1,0:T(8,128)(2,1)} %convolution_convert_fusion.3) | copy-start | bytes 3145732
  106.7 17.0 %collective-permute-start.7 = (bf16[256,128]{1,0:T(8,128)(2,1)S(1)}, bf16[256,128]{1,0:T(8,128)(2,1)S(1)}, u32[]{:S(2)}, u32[]{:S(2)}) collective-permute-start(bf16[256,128]{1,0:T(8,128)(2,1)S(1)} %dynamic-slice_bitcast_fusion), channel_id=1, source_target_pairs={{0,8},{8,0},{16,24},{24,16},{1,9},{9,1},{17,25},{25,17},{2,10},{10... | collective-permute-start | bytes 196616 | tf_op jit(solution)/shard_map/ppermute | solution.py:22
  108.1 4.7 %copy-start.10 = (bf16[16,128,256]{2,1,0:T(8,128)(2,1)S(1)}, bf16[16,128,256]{2,1,0:T(8,128)(2,1)}, u32[]{:S(2)}) copy-start(bf16[16,128,256]{2,1,0:T(8,128)(2,1)} %fusion.144) | copy-start | bytes 3145732
  112.8 4.7 %copy-start.5 = (bf16[1,256,1024]{2,1,0:T(8,128)(2,1)S(1)}, bf16[1,256,1024]{2,1,0:T(8,128)(2,1)}, u32[]{:S(2)}) copy-start(bf16[1,256,1024]{2,1,0:T(8,128)(2,1)} %param.12) | copy-start | bytes 1572868
  117.5 4.9 %copy-start.33 = (bf16[1,1024,2048]{2,1,0:T(8,128)(2,1)S(1)}, bf16[1,1024,2048]{2,1,0:T(8,128)(2,1)}, u32[]{:S(2)}) copy-start(bf16[1,1024,2048]{2,1,0:T(8,128)(2,1)} %param.16) | copy-start | bytes 12582916
  117.5 4.9 %copy-start.43 = (f32[256,1024]{1,0:T(8,128)S(1)}, f32[256,1024]{1,0:T(8,128)}, u32[]{:S(2)}) copy-start(f32[256,1024]{1,0:T(8,128)} %fusion.18) | copy-start | bytes 3145732
  122.4 3.7 %copy-start.9 = (bf16[16,128,256]{2,1,0:T(8,128)(2,1)S(1)}, bf16[16,128,256]{2,1,0:T(8,128)(2,1)}, u32[]{:S(2)}) copy-start(bf16[16,128,256]{2,1,0:T(8,128)(2,1)} %convolution_convert_fusion.3) | copy-start | bytes 3145732
  122.4 3.7 %copy-start.38 = (bf16[1,1024,2048]{2,1,0:T(8,128)(2,1)S(1)}, bf16[1,1024,2048]{2,1,0:T(8,128)(2,1)}, u32[]{:S(2)}) copy-start(bf16[1,1024,2048]{2,1,0:T(8,128)(2,1)} %param.18) | copy-start | bytes 12582916
  123.8 6.5 %collective-permute-start.8 = (bf16[256,128]{1,0:T(8,128)(2,1)S(1)}, bf16[256,128]{1,0:T(8,128)(2,1)S(1)}, u32[]{:S(2)}, u32[]{:S(2)}) collective-permute-start(bf16[256,128]{1,0:T(8,128)(2,1)S(1)} %collective-permute-done.7), channel_id=1, source_target_pairs={{0,16},{8,24},{16,0},{24,8},{1,17},{9,25},{17,1},{25,9},{2,18},{10... | collective-permute-start | bytes 196616 | tf_op jit(solution)/shard_map/ppermute | solution.py:22
  128.5 204.5 %all-reduce.5.cloned.1.call-start = ((), (), s32[]{:S(2)}) async-start(), calls=%async_computation | async-start | bytes 4194304 | tf_op jit(solution)/shard_map/psum | solution.py:64
  128.5 18.4 %copy-start.34 = (bf16[1,1024,2048]{2,1,0:T(8,128)(2,1)S(1)}, bf16[1,1024,2048]{2,1,0:T(8,128)(2,1)}, u32[]{:S(2)}) copy-start(bf16[1,1024,2048]{2,1,0:T(8,128)(2,1)} %param.16) | copy-start | bytes 12582916
  189.7 6.7 %copy-start = (f32[256,1024]{1,0:T(8,128)S(1)}, f32[256,1024]{1,0:T(8,128)}, u32[]{:S(2)}) copy-start(f32[256,1024]{1,0:T(8,128)} %get-tuple-element.15) | copy-start | bytes 3145732
  189.7 15.1 %copy-start.11 = (bf16[2,256,1024]{2,1,0:T(8,128)(2,1)S(1)}, bf16[2,256,1024]{2,1,0:T(8,128)(2,1)}, u32[]{:S(2)}) copy-start(bf16[2,256,1024]{2,1,0:T(8,128)(2,1)} %param.13) | copy-start | bytes 3145732
  189.7 15.3 %copy-start.35 = (bf16[1,1024,2048]{2,1,0:T(8,128)(2,1)S(1)}, bf16[1,1024,2048]{2,1,0:T(8,128)(2,1)}, u32[]{:S(2)}) copy-start(bf16[1,1024,2048]{2,1,0:T(8,128)(2,1)} %param.16) | copy-start | bytes 12582916
  191.2 13.5 %collective-permute-start = (bf16[256,1024]{1,0:T(8,128)(2,1)S(1)}, bf16[256,1024]{1,0:T(8,128)(2,1)S(1)}, u32[]{:S(2)}, u32[]{:S(2)}) collective-permute-start(bf16[256,1024]{1,0:T(8,128)(2,1)S(1)} %fusion.201), channel_id=1, source_target_pairs={{0,8},{8,16},{16,24},{1,9},{9,17},{17,25},{2,10},{10,18},{18,26},{... | collective-permute-start | bytes 1572872 | tf_op jit(solution)/shard_map/ppermute | solution.py:16
  196.8 10.6 %copy-start.30 = (bf16[1,1024,2048]{2,1,0:T(8,128)(2,1)S(1)}, bf16[1,1024,2048]{2,1,0:T(8,128)(2,1)}, u32[]{:S(2)}) copy-start(bf16[1,1024,2048]{2,1,0:T(8,128)(2,1)} %param.17) | copy-start | bytes 12582916
  196.8 15.3 %collective-permute-start.4 = (bf16[256,1024]{1,0:T(8,128)(2,1)S(1)}, bf16[256,1024]{1,0:T(8,128)(2,1)S(1)}, u32[]{:S(2)}, u32[]{:S(2)}) collective-permute-start(bf16[256,1024]{1,0:T(8,128)(2,1)S(1)} %fusion.189), channel_id=1, source_target_pairs={{8,0},{16,8},{24,16},{9,1},{17,9},{25,17},{10,2},{18,10},{26,18},{... | collective-permute-start | bytes 1572872 | tf_op jit(solution)/shard_map/ppermute | solution.py:16
  205.0 4.7 %copy-start.1 = (bf16[256,1024]{1,0:T(8,128)(2,1)}, bf16[256,1024]{1,0:T(8,128)(2,1)S(1)}, u32[]{:S(2)}) copy-start(bf16[256,1024]{1,0:T(8,128)(2,1)S(1)} %get-tuple-element.17) | copy-start | bytes 1572868
  209.8 2.9 copy-start.25
  216.4 3.4 copy-start.41
  221.7 8.4 %copy-start.16 = (bf16[256,2048]{0,1:T(8,128)(2,1)S(1)}, bf16[256,2048]{0,1:T(8,128)(2,1)}, u32[]{:S(2)}) copy-start(bf16[256,2048]{0,1:T(8,128)(2,1)} %copy.67) | copy-start | bytes 3145732
  230.0 10.8 %copy-start.18 = (bf16[256,2048]{1,0:T(8,128)(2,1)S(1)}, bf16[256,2048]{1,0:T(8,128)(2,1)}, u32[]{:S(2)}) copy-start(bf16[256,2048]{1,0:T(8,128)(2,1)} %fusion.75) | copy-start | bytes 3145732
  238.3 47.2 %collective-permute-start.10 = (bf16[256,128]{1,0:T(8,128)(2,1)S(1)}, bf16[256,128]{1,0:T(8,128)(2,1)S(1)}, u32[]{:S(2)}, u32[]{:S(2)}) collective-permute-start(bf16[256,128]{1,0:T(8,128)(2,1)S(1)} %constant_dynamic-slice_fusion), channel_id=1, source_target_pairs={{0,8},{8,0},{16,24},{24,16},{1,9},{9,1},{17,25},{25,17},{2,10},{10... | collective-permute-start | bytes 196616 | tf_op jit(solution)/shard_map/ppermute | solution.py:22
  247.4 4.0 %copy-start.19 = (bf16[16,128,256]{2,1,0:T(8,128)(2,1)S(1)}, bf16[16,128,256]{2,1,0:T(8,128)(2,1)}, u32[]{:S(2)}) copy-start(bf16[16,128,256]{2,1,0:T(8,128)(2,1)} %fusion.141) | copy-start | bytes 3145732
  247.4 4.0 %copy-start.31 = (bf16[1,1024,2048]{2,1,0:T(8,128)(2,1)S(1)}, bf16[1,1024,2048]{2,1,0:T(8,128)(2,1)}, u32[]{:S(2)}) copy-start(bf16[1,1024,2048]{2,1,0:T(8,128)(2,1)} %param.17) | copy-start | bytes 12582916
  251.4 2.5 copy-start.36
  252.7 3.0 copy-start.40
  258.0 7.0 %copy-start.22 = (bf16[16,128,256]{2,1,0:T(8,128)(2,1)S(1)}, bf16[16,128,256]{2,1,0:T(8,128)(2,1)}, u32[]{:S(2)}) copy-start(bf16[16,128,256]{2,1,0:T(8,128)(2,1)} %fusion.138) | copy-start | bytes 3145732
  271.8 7.0 %copy-start.7 = (bf16[16,128,256]{2,1,0:T(8,128)(2,1)S(1)}, bf16[16,128,256]{2,1,0:T(8,128)(2,1)}, u32[]{:S(2)}) copy-start(bf16[16,128,256]{2,1,0:T(8,128)(2,1)} %convolution_convert_fusion) | copy-start | bytes 3145732
  285.5 52.1 %copy-start.2 = (bf16[256,1024]{1,0:T(8,128)(2,1)S(1)}, bf16[256,1024]{1,0:T(8,128)(2,1)}, u32[]{:S(2)}) copy-start(bf16[256,1024]{1,0:T(8,128)(2,1)} %copy-done.1) | copy-start | bytes 1572868
  285.5 66.6 %copy-start.12 = (bf16[2,256,1024]{2,1,0:T(8,128)(2,1)S(1)}, bf16[2,256,1024]{2,1,0:T(8,128)(2,1)}, u32[]{:S(2)}) copy-start(bf16[2,256,1024]{2,1,0:T(8,128)(2,1)} %param.13) | copy-start | bytes 3145732
  285.5 56.9 %collective-permute-start.11 = (bf16[256,128]{1,0:T(8,128)(2,1)S(1)}, bf16[256,128]{1,0:T(8,128)(2,1)S(1)}, u32[]{:S(2)}, u32[]{:S(2)}) collective-permute-start(bf16[256,128]{1,0:T(8,128)(2,1)S(1)} %collective-permute-done.10), channel_id=1, source_target_pairs={{0,16},{8,24},{16,0},{24,8},{1,17},{9,25},{17,1},{25,9},{2,18},{10... | collective-permute-start | bytes 196616 | tf_op jit(solution)/shard_map/ppermute | solution.py:22
  333.0 4.7 %copy-start.17 = (f32[256,1024]{1,0:T(8,128)S(1)}, f32[256,1024]{1,0:T(8,128)}, u32[]{:S(2)}) copy-start(f32[256,1024]{1,0:T(8,128)} %get-tuple-element.12) | copy-start | bytes 3145732
  333.0 17.8 %copy-start.14 = (bf16[2,256,1024]{2,1,0:T(8,128)(2,1)S(1)}, bf16[2,256,1024]{2,1,0:T(8,128)(2,1)}, u32[]{:S(2)}) copy-start(bf16[2,256,1024]{2,1,0:T(8,128)(2,1)} %param.14) | copy-start | bytes 3145732
  336.4 14.4 %collective-permute-start.9 = (bf16[256,1024]{1,0:T(8,128)(2,1)S(1)}, bf16[256,1024]{1,0:T(8,128)(2,1)S(1)}, u32[]{:S(2)}, u32[]{:S(2)}) collective-permute-start(bf16[256,1024]{1,0:T(8,128)(2,1)S(1)} %fusion.197), channel_id=1, source_target_pairs={{8,0},{16,8},{24,16},{9,1},{17,9},{25,17},{10,2},{18,10},{26,18},{... | collective-permute-start | bytes 1572872 | tf_op jit(solution)/shard_map/ppermute | solution.py:16
  337.8 14.3 %collective-permute-start.1 = (bf16[256,1024]{1,0:T(8,128)(2,1)S(1)}, bf16[256,1024]{1,0:T(8,128)(2,1)S(1)}, u32[]{:S(2)}, u32[]{:S(2)}) collective-permute-start(bf16[256,1024]{1,0:T(8,128)(2,1)S(1)} %fusion.207), channel_id=1, source_target_pairs={{0,8},{8,16},{16,24},{1,9},{9,17},{17,25},{2,10},{10,18},{18,26},{... | collective-permute-start | bytes 1572872 | tf_op jit(solution)/shard_map/ppermute | solution.py:16
  342.5 10.5 %copy-start.23 = (bf16[1,4,256,128]{3,2,1,0:T(8,128)(2,1)}, bf16[1,4,256,128]{3,2,1,0:T(8,128)(2,1)S(1)}, u32[]{:S(2)}) copy-start(bf16[1,4,256,128]{3,2,1,0:T(8,128)(2,1)S(1)} %bitcast_dynamic-update-slice_fusion) | copy-start | bytes 786436
  (10 other events, 21.9 us)
Sparse Core Ops, SparseCore 0:
  128.6 61.0 all-reduce.6
  271.9 60.9 all-reduce.4
where the time goes:
time: 367 us; the launch traced here: 360 us
  matrix products  165 us (45%)
  waiting for transfers between devices  84.4 us (23%)
  starting transfers between devices  26.2 us (7%)
  local copies, waits for them, and re-layouts  24.6 us (7%)
  blocking collectives  22.7 us (6%)
  between operations  18.7 us (5%)
  other arithmetic  18 us (5%)
    psum x2, waiting for transfers between devices, ahead(): total = lax.psum(partial_value, 'head')  68.2 us
    all_gather x2, blocking collectives, per_device(): restored = lax.all_gather(reloaded, 'head', axis=1, tiled=True)  22.7 us
    dot_general x2, matrix products, behind(): jnp.einsum('hqk,khd->qhd', score_grad, split_heads(key_rows), preferred_e...  16.9 us
    dot_general x2, matrix products, behind(): jnp.einsum('hqk,qhd->khd', score_grad, split_heads(queries), preferred_el...  15.9 us
    reshape x10, local copies, waits for them, and re-layouts, split_heads(): return rows.reshape(rows.shape[0], -1, DK)  15.1 us
    ppermute x8, starting transfers between devices, swapped(): return lax.ppermute(value, axis, pairs)  15 us
    ppermute x4, waiting for transfers between devices, passed_along(): return lax.ppermute(value, axis, pairs)  14.4 us
    dot_general x4, matrix products, attend(): jnp.dot(normed, value_part, preferred_element_type=jnp.float32)  12.7 us
  transfers between devices with their start and end apart: 14, of which 6 were waited for; matrix products, arithmetic and copies ran while one was open for 48% of the time, Pallas kernels for 0%

commit v1 on v0

v1 whole, which is shorter than its diff:
```python
import functools

import jax
import jax.numpy as jnp
from jax import lax
from jax.experimental import pallas as pl
from jax.experimental.pallas import tpu as pltpu
from jax.sharding import PartitionSpec as P

DK = 128
TICKS = 2


epsilon = 1e-06
ONES = (((1,), (1,)), ((), ()))
ZEROS = (((0,), (0,)), ((), ()))


def passed_along(value, axis, by):
    count = lax.axis_size(axis)
    pairs = [(i, i + by) for i in range(count) if 0 <= i + by < count]
    return lax.ppermute(value, axis, pairs)


def mirrored(value, axis):
    count = lax.axis_size(axis)
    return lax.ppermute(value, axis, [(i, count - 1 - i) for i in range(count)])


def normalize(rows, gain_row):
    floats = rows.astype(jnp.float32)
    inverse = lax.rsqrt(jnp.mean(floats * floats, axis=-1, keepdims=True) + epsilon)
    unit_rows = floats * inverse
    return ((unit_rows * gain_row).astype(jnp.bfloat16), unit_rows, inverse)


def dot(a, b, dims=(((1,), (0,)), ((), ()))):
    return lax.dot_general(a, b, dims, preferred_element_type=jnp.float32)


def low_dot(a, b, dims=(((1,), (0,)), ((), ()))):
    return dot(a, b, dims).astype(jnp.bfloat16)


def softmax_of(queries, key_rows):
    scores = dot(queries, key_rows, ONES) * DK ** (-0.5)
    exponent = jnp.exp(scores - jnp.max(scores, axis=-1, keepdims=True))
    return exponent * (1.0 / jnp.sum(exponent, axis=-1, keepdims=True))


def forward_kernel(rows, gain, wq, wk, wv, wo, total, normed):
    step = pl.program_id(0)

    @pl.when(step == 0)
    def _():
        normed[...] = normalize(rows[...], gain[...])[0]
        total[...] = jnp.zeros_like(total)

    n = normed[...]
    queries, key_rows, value_rows = low_dot(n, wq[...]), low_dot(n, wk[...]), low_dot(n, wv[...])
    parts = []
    for start in range(0, queries.shape[1], DK):
        head = slice(start, start + DK)
        soft = softmax_of(queries[:, head], key_rows[:, head]).astype(jnp.bfloat16)
        parts.append(low_dot(soft, value_rows[:, head]))
    total[...] += dot(jnp.concatenate(parts, axis=1), wo[...])


def backward_kernel(rows, upstream, gain, wq, wk, wv, wo, total, normed, ctx, qg, kg, vg):
    step = pl.program_id(0)

    @pl.when(step == 0)
    def _():
        normed[...] = normalize(rows[...], gain[...])[0]
        total[...] = jnp.zeros_like(total)

    n = normed[...]
    queries, key_rows, value_rows = low_dot(n, wq[...]), low_dot(n, wk[...]), low_dot(n, wv[...])
    ctx_grad = low_dot(upstream[...], wo[...], ONES)
    for start in range(0, queries.shape[1], DK):
        head = slice(start, start + DK)
        q, k, v, c = queries[:, head], key_rows[:, head], value_rows[:, head], ctx_grad[:, head]
        soft = softmax_of(q, k)
        soft_low = soft.astype(jnp.bfloat16)
        ctx[:, head] = low_dot(soft_low, v)
        soft_grad = dot(c, v, ONES)
        vg[:, head] = low_dot(soft_low, c, ZEROS)
        inner = jnp.sum(soft * soft_grad, axis=-1, keepdims=True)
        score_grad = (soft * (soft_grad - inner) * DK ** (-0.5)).astype(jnp.bfloat16)
        qg[:, head] = low_dot(score_grad, k)
        kg[:, head] = low_dot(score_grad, q, ZEROS)
    total[...] += (
        dot(qg[...], wq[...], ONES) + dot(kg[...], wk[...], ONES) + dot(vg[...], wv[...], ONES)
    )


def gradient_kernel(
    n0, n1, g0, g1, c0, c1, q0, q1, k0, k1, v0, v1, wq, wk, wv, wo, turned, upstream
):
    @pl.when(pl.program_id(0) == 0)
    def _():
        count = n0.shape[0]
        turned[:, :count] = n0[...].T
        turned[:, count:] = n1[...].T
        upstream[:count] = g0[...]
        upstream[count:] = g1[...]

    def both(first, second):
        return jnp.concatenate([first[...], second[...]], axis=0)

    wq[...] = low_dot(turned[...], both(q0, q1))
    wk[...] = low_dot(turned[...], both(k0, k1))
    wv[...] = low_dot(turned[...], both(v0, v1))
    wo[...] = low_dot(both(c0, c1), upstream[...], ZEROS)


def whole(shape):
    return pl.BlockSpec(shape, lambda i: (0,) * len(shape))


def columns(rows, width):
    return pl.BlockSpec((rows, width), lambda i: (0, i))


def row_blocks(width, columns_):
    return pl.BlockSpec((width, columns_), lambda i: (i, 0))


PARAMS = dict(dimension_semantics=("arbitrary",), vmem_limit_bytes=56 * 2**20)


def weight_specs(depth, width):
    return [columns(depth, width)] * 3 + [row_blocks(width, depth)]


def step_width(inner):
    return 4 * DK if inner % (4 * DK) == 0 else DK


def forward_part(rows, weights):
    count, depth = rows.shape
    inner = weights[1].shape[1]
    width = step_width(inner)
    return pl.pallas_call(
        forward_kernel,
        grid=(inner // width,),
        in_specs=[whole((count, depth)), whole((1, depth))] + weight_specs(depth, width),
        out_specs=whole((count, depth)),
        out_shape=jax.ShapeDtypeStruct((count, depth), jnp.float32),
        scratch_shapes=[pltpu.VMEM((count, depth), jnp.bfloat16)],
        compiler_params=pltpu.CompilerParams(**PARAMS),
        cost_estimate=pl.CostEstimate(
            flops=8 * count * depth * inner + 4 * count * count * inner,
            bytes_accessed=8 * depth * inner,
            transcendentals=count * count * inner // DK,
        ),
    )(rows, *weights)


def backward_part(rows, upstream, weights):
    count, depth = rows.shape
    inner = weights[1].shape[1]
    width = step_width(inner)
    wide = jax.ShapeDtypeStruct((count, inner), jnp.bfloat16)
    return pl.pallas_call(
        backward_kernel,
        grid=(inner // width,),
        in_specs=[whole((count, depth)), whole((count, depth)), whole((1, depth))]
        + weight_specs(depth, width),
        out_specs=[whole((count, depth)), whole((count, depth))] + [columns(count, width)] * 4,
        out_shape=[
            jax.ShapeDtypeStruct((count, depth), jnp.float32),
            jax.ShapeDtypeStruct((count, depth), jnp.bfloat16),
        ]
        + [wide] * 4,
        compiler_params=pltpu.CompilerParams(**PARAMS),
        cost_estimate=pl.CostEstimate(
            flops=14 * count * depth * inner + 12 * count * count * inner,
            bytes_accessed=8 * depth * inner,
            transcendentals=count * count * inner // DK,
        ),
    )(rows, upstream, *weights)


def gradients(first, second, g0, g1):
    n0, c0, q0, k0, v0 = first
    n1, c1, q1, k1, v1 = second
    count, depth = n0.shape
    inner = q0.shape[1]
    width = step_width(inner)
    low = jnp.bfloat16
    return pl.pallas_call(
        gradient_kernel,
        grid=(inner // width,),
        in_specs=[whole((count, depth))] * 4 + [columns(count, width)] * 8,
        out_specs=weight_specs(depth, width),
        out_shape=[jax.ShapeDtypeStruct((depth, inner), low)] * 3
        + [jax.ShapeDtypeStruct((inner, depth), low)],
        scratch_shapes=[
            pltpu.VMEM((depth, 2 * count), low),
            pltpu.VMEM((2 * count, depth), low),
        ],
        compiler_params=pltpu.CompilerParams(**PARAMS),
        cost_estimate=pl.CostEstimate(
            flops=16 * count * depth * inner, bytes_accessed=8 * depth * inner, transcendentals=0
        ),
    )(n0, n1, g0, g1, c0, c1, q0, q1, k0, k1, v0, v1)


def sent_forward(rows, part):
    total = lax.psum(part, "head")
    return passed_along((rows.astype(jnp.float32) + total).astype(jnp.bfloat16), "section", 1)


def sent_back(rows, upstream, gain_row, part):
    normed, unit_rows, inverse = normalize(rows, gain_row)
    normed_grad = lax.psum(part, "head")
    gain_full = jnp.sum(normed_grad * unit_rows, axis=0)
    unit_grad = normed_grad * gain_row
    along = jnp.mean(unit_grad * unit_rows, axis=-1, keepdims=True)
    returned = upstream.astype(jnp.float32) + inverse * (unit_grad - unit_rows * along)
    return passed_along(returned.astype(jnp.bfloat16), "section", -1), gain_full


def per_device(
    section_inputs,
    section_cotangents,
    fresh_tokens,
    fresh_cotangents,
    norm_gain,
    query_weight,
    key_weight,
    value_weight,
    out_weight,
    saved_inputs,
    reload_slot,
):
    section_count = lax.axis_size("section")
    section_index = lax.axis_index("section")
    head_index = lax.axis_index("head")
    mirror_index = section_count - 1 - section_index
    share_width = saved_inputs.shape[3]
    column_start = head_index * share_width
    weights = (norm_gain, query_weight[0], key_weight[0], value_weight[0], out_weight[0])
    x0 = section_inputs[0]
    g0 = section_cotangents[0]
    store = saved_inputs[0]
    count = x0.shape[0]

    def own_share(block):
        return lax.dynamic_slice_in_dim(block, column_start, share_width, 1)

    held = lax.dynamic_index_in_dim(reload_slot, mirror_index, 1, keepdims=False)
    held0 = lax.dynamic_index_in_dim(store, held[0], 0, keepdims=False)
    held1 = lax.dynamic_index_in_dim(store, held[1], 0, keepdims=False)
    own = lax.dynamic_index_in_dim(reload_slot, section_index, 1, keepdims=False)

    travel = mirrored(jnp.concatenate([own_share(x0), held0, held1], axis=0), "section")
    arrived, reloads = travel[:count], travel[count:]
    restored = lax.all_gather(reloads, "head", axis=1, tiled=True)
    b0 = restored[:count]
    b1 = jnp.where(own[0] == own[1], x0, restored[count:])

    part = forward_part(x0, weights)
    x1 = jnp.where(section_index == 0, fresh_tokens[0], sent_forward(x0, part))

    part, *first = backward_part(b0, g0, weights)
    moved, gain0 = sent_back(b0, g0, norm_gain, part)
    g1 = jnp.where(section_index == section_count - 1, fresh_cotangents[0], moved)

    part = forward_part(x1, weights)
    x2 = jnp.where(section_index == 0, fresh_tokens[1], sent_forward(x1, part))
    arrived1 = mirrored(own_share(x1), "section")
    store = lax.dynamic_update_index_in_dim(store, arrived, held[0], 0)
    store = lax.dynamic_update_index_in_dim(store, arrived1, held[1], 0)

    part, *second = backward_part(b1, g1, weights)
    moved, gain1 = sent_back(b1, g1, norm_gain, part)
    g2 = jnp.where(section_index == section_count - 1, fresh_cotangents[1], moved)

    grads = gradients(first, second, g0, g1)
    gain = lax.dynamic_slice_in_dim(gain0 + gain1, column_start, share_width, 0)
    return (x2[None], g2[None], store[None], *(grad[None] for grad in grads), gain[None])


def solution(mesh):
    placed = (
        P("section", None, None),
        P("section", None, None),
        P(),
        P(),
        P("section", None),
        P("section", None, "head"),
        P("section", None, "head"),
        P("section", None, "head"),
        P("section", "head", None),
        P("section", None, None, "head"),
        P(),
    )
    return jax.shard_map(
        per_device,
        mesh=mesh,
        in_specs=placed,
        out_specs=(
            P("section", None, None),
            P("section", None, None),
            P("section", None, None, "head"),
            P("section", None, "head"),
            P("section", None, "head"),
            P("section", None, "head"),
            P("section", "head", None),
            P("section", "head"),
        ),
        check_vma=False,
    )
```

time: 367 us -> 281 us (0.77); the launches traced: 360 us -> 280 us
  matrix products: 165 us -> 0 us
  Pallas kernels: 0 us -> 81.1 us
  waiting for transfers between devices: 84.4 us -> 140 us
  blocking collectives: 22.7 us -> 0 us
  local copies, waits for them, and re-layouts: 24.6 us -> 7.92 us
  other arithmetic: 18 us -> 12 us
  starting transfers between devices: 26.2 us -> 20.2 us
    dot_general x44 -> x0, matrix products: 155 us -> none  [the longest x2 16.9 us: behind(): jnp.einsum('hqk,khd->qhd', score_grad, split_heads(key_rows), preferred_e...]
    pallas_call x0 -> x5, Pallas kernels: none -> 81.1 us  [the longest x2 42.3 us: backward_part(): pl.pallas_call(backward_kernel, grid=(inner // width,), in_specs=[whole((...]
    psum x2, waiting for transfers between devices: 68.2 us -> 105 us  [sent_forward(): total = lax.psum(part, 'head')]
    all_gather x2 -> x0, blocking collectives: 22.7 us -> none  [per_device(): restored = lax.all_gather(reloaded, 'head', axis=1, tiled=True)]
    reshape x10 -> x0, local copies, waits for them, and re-layouts: 15.1 us -> none  [split_heads(): return rows.reshape(rows.shape[0], -1, DK)]
    all_gather x0 -> x1, waiting for transfers between devices: none -> 13.8 us  [per_device(): restored = lax.all_gather(reloads, 'head', axis=1, tiled=True)]
    sub x2 -> x0, matrix products: 10.2 us -> none  [attend(): exponent = jnp.exp(scores - highest)]
    sub x2 -> x0, other arithmetic: 6.45 us -> none  [attend(): exponent = jnp.exp(scores - highest)]
  transfers between devices with their start and end apart: 14 -> 9, of which waited for: 6 -> 7; matrix products, arithmetic and copies ran while one was open for 48% -> 2% of each run, Pallas kernels for 0% -> 14%
where the time goes in v1:
time: 281 us; the launch traced here: 280 us
  waiting for transfers between devices  140 us (50%)
  Pallas kernels  81.1 us (29%)
  starting transfers between devices  20.2 us (7%)
  between operations  19.3 us (7%)
  other arithmetic  12 us (4%)
  local copies, waits for them, and re-layouts  7.92 us (3%)
    psum x2, waiting for transfers between devices, sent_forward(): total = lax.psum(part, 'head')  105 us
    pallas_call x2, Pallas kernels, backward_part(): pl.pallas_call(backward_kernel, grid=(inner // width,), in_specs=[whole((...  42.3 us
    pallas_call x2, Pallas kernels, forward_part(): pl.pallas_call(forward_kernel, grid=(inner // width,), in_specs=[whole((c...  24.5 us
    ppermute x4, waiting for transfers between devices, passed_along(): return lax.ppermute(value, axis, pairs)  16.2 us
    pallas_call x1, Pallas kernels, gradients(): pl.pallas_call(gradient_kernel, grid=(inner // width,), in_specs=[whole((...  14.3 us
    all_gather x1, waiting for transfers between devices, per_device(): restored = lax.all_gather(reloads, 'head', axis=1, tiled=True)  13.8 us
    ppermute x4, starting transfers between devices, passed_along(): return lax.ppermute(value, axis, pairs)  10.7 us
    ppermute x2, starting transfers between devices, mirrored(): return lax.ppermute(value, axis, [(i, count - 1 - i) for i in range(count)])  9.44 us
  transfers between devices with their start and end apart: 9, of which 7 were waited for; matrix products, arithmetic and copies ran while one was open for 2% of the time, Pallas kernels for 14%

profile of v1, /device:TPU:0, one launch (start us, length us, event | category | flops | bytes accessed | tf_op | source)
XLA Modules:
  0.0 280.2 jit_solution(3724909584480451990)
XLA Ops:
  7.2 0.0 all-gather.2.cloned.1.call-start
  7.2 1.0 copy.26
  8.2 0.8 constant_dynamic-slice_fusion.1
  9.0 0.5 fusion.23
  13.4 0.8 dynamic-slice_bitcast_fusion.2
  14.3 5.1 %collective-permute-start.2 = (bf16[768,128]{1,0:T(8,128)(2,1)S(1)}, bf16[768,128]{1,0:T(8,128)(2,1)S(1)}, u32[]{:S(2)}, u32[]{:S(2)}) collective-permute-start(bf16[768,128]{1,0:T(8,128)(2,1)S(1)} %pad_maximum_fusion), channel_id=1, source_target_pairs={{0,24},{8,16},{16,8},{24,0},{1,25},{9,17},{17,9},{25,1},{2,26},{10... | collective-permute-start | bytes 589832 | tf_op jit(solution)/shard_map/ppermute | solution.py:27
  19.4 5.0 %collective-permute-done.2 = bf16[768,128]{1,0:T(8,128)(2,1)S(1)} collective-permute-done((bf16[768,128]{1,0:T(8,128)(2,1)S(1)}, bf16[768,128]{1,0:T(8,128)(2,1)S(1)}, u32[]{:S(2)}, u32[]{:S(2)}) %collective-permute-start.2) | collective-permute-done | bytes 196640 | tf_op jit(solution)/shard_map/ppermute | solution.py:27
  24.4 0.7 copy-done.11
  25.1 0.7 slice.54
  25.8 0.0 all-gather.2.cloned.1.call-update
  25.8 0.0 all-reduce.7.cloned.1.call-start
  25.9 12.2 %shard_map.170 = f32[256,1024]{1,0:T(8,128)} custom-call(bf16[256,1024]{1,0:T(8,128)(2,1)} %bitcast.64, f32[1,1024]{1,0:T(1,128)} %gain.7, bf16[1024,2048]{1,0:T(8,128)(2,1)} %bitcast.48, bf16[1024,2048]{1,0:T(8,128)(2,1)} %bitcast.52, bf16[1024,2048]{1,0:T(8,128)(2,1)} %bitcast.56, bf16[2048,1024]{1,0:T(8,128)(2,1)} %bitcast.60), custom_call_target="tpu_custom_call" | custom-call | flops 4831838208 | bytes 16777216 | tf_op jit(solution)/shard_map/pallas_call | solution.py:144
  38.1 13.8 %all-gather.2.cloned.1.call-done = bf16[512,1024]{1,0:T(8,128)(2,1)} async-done(((bf16[512,128]{1,0:T(8,128)(2,1)}), bf16[512,1024]{1,0:T(8,128)(2,1)}) %all-gather.2.cloned.1.call-update) | async-done | bytes 1048592 | tf_op jit(solution)/shard_map/all_gather | solution.py:260
  51.9 1.9 slice.55.rows
  53.8 21.1 %shard_map.172 = (f32[256,1024]{1,0:T(8,128)}, bf16[256,1024]{1,0:T(8,128)(2,1)}, bf16[256,2048]{1,0:T(8,128)(2,1)}, bf16[256,2048]{1,0:T(8,128)(2,1)}, bf16[256...) custom-call(bf16[256,1024]{1,0:T(8,128)(2,1)} %slice.55.rows, bf16[256,1024]{1,0:T(8,128)(2,1)} %bitcast.65, f32[1,1024]{1,0:T(1,128)} %gain.7, ...), custom_call_target="tpu_custom_call" | custom-call | flops 9126805504 | bytes 16777216 | tf_op jit(solution)/shard_map/pallas_call | solution.py:165
  74.9 0.0 copy-start.3
  74.9 0.0 copy-start.10
  74.9 0.0 all-reduce.7.cloned.1.call-update
  75.0 0.0 copy-start.6
  75.0 0.0 all-reduce.5.cloned.1.call-start
  76.5 0.2 fusion.12
  76.7 60.3 %all-reduce.7.cloned.1.call-done = (f32[256,1024]{1,0:T(8,128)}, f32[256,1024]{1,0:T(8,128)}) async-done(((f32[256,1024]{1,0:T(8,128)}, f32[256,1024]{1,0:T(8,128)}), (f32[256,1024]{1,0:T(8,128)}, f32[256,1024]{1,0:T(8,128)})) %all-reduce.7.cloned.1.call-update) | async-done | bytes 2097168 | tf_op jit(solution)/shard_map/psum | solution.py:211
  136.9 1.7 fusion.11
  138.6 3.1 %fusion.19 = (f32[256]{0:T(256)S(1)}, bf16[256,1024]{1,0:T(8,128)(2,1)}, bf16[256,1024]{1,0:T(8,128)(2,1)}, bf16[256,1024]{1,0:T(8,128)(2,1)}) fusion(bf16[512,1024]{1,0:T(8,128)(2,1)S(1)} %copy-done, bf16[1,256,1024]{2,1,0:T(8,128)(2,1)S(1)} %copy-done.3, pred[]{:T(512)} %bitcast.17, f32[256]{0:T(256)S(1)} %broadcast_multiply_fusion.1, ...), kind=kLoop, calls=%fused_computation.23 | loop fusion | flops 4194048 | bytes 5774337 | tf_op jit(solution)/shard_map/reduce_sum | solution.py:32
  141.7 3.3 %collective-permute-start = (bf16[256,1024]{1,0:T(8,128)(2,1)}, bf16[256,1024]{1,0:T(8,128)(2,1)S(1)}, u32[]{:S(2)}, u32[]{:S(2)}) collective-permute-start(bf16[256,1024]{1,0:T(8,128)(2,1)} %get-tuple-element.51), channel_id=1, source_target_pairs={{0,8},{8,16},{16,24},{1,9},{9,17},{17,25},{2,10},{10,18},{18,26},{... | collective-permute-start | bytes 1572872 | tf_op jit(solution)/shard_map/ppermute | solution.py:22
  145.1 0.9 fusion.22
  145.9 1.5 collective-permute-start.3
  147.4 8.0 %collective-permute-done = bf16[256,1024]{1,0:T(8,128)(2,1)S(1)} collective-permute-done((bf16[256,1024]{1,0:T(8,128)(2,1)}, bf16[256,1024]{1,0:T(8,128)(2,1)S(1)}, u32[]{:S(2)}, u32[]{:S(2)}) %collective-permute-start) | collective-permute-done | bytes 524320 | tf_op jit(solution)/shard_map/ppermute | solution.py:22
  155.4 0.8 bitcast_select_fusion.2.rows
  156.3 12.3 %shard_map.171 = f32[256,1024]{1,0:T(8,128)} custom-call(bf16[256,1024]{1,0:T(8,128)(2,1)} %bitcast_select_fusion.2.rows, f32[1,1024]{1,0:T(1,128)} %gain.7, bf16[1024,2048]{1,0:T(8,128)(2,1)} %bitcast.50, bf16[1024,2048]{1,0:T(8,128)(2,1)} %bitcast.54, bf16[1024,2048]{1,0:T(8,128)(2,1)} %bitcast.58, bf16[2048,1024]{1,0:T(8,128)(2,1)} %bitcast.62), custom_call_target="tpu_custom_call" | custom-call | flops 4831838208 | bytes 16777216 | tf_op jit(solution)/shard_map/pallas_call | solution.py:144
  168.6 0.9 bitcast_select_fusion.upstream.g1
  169.5 21.2 %shard_map.173 = (f32[256,1024]{1,0:T(8,128)}, bf16[256,1024]{1,0:T(8,128)(2,1)}, bf16[256,2048]{1,0:T(8,128)(2,1)}, bf16[256,2048]{1,0:T(8,128)(2,1)}, bf16[256...) custom-call(bf16[256,1024]{1,0:T(8,128)(2,1)} %get-tuple-element.49.rows, bf16[256,1024]{1,0:T(8,128)(2,1)} %bitcast_select_fusion.upstream.g1, ...), custom_call_target="tpu_custom_call" | custom-call | flops 9126805504 | bytes 16777216 | tf_op jit(solution)/shard_map/pallas_call | solution.py:165
  190.7 0.0 all-reduce.5.cloned.1.call-update
  190.7 4.3 %collective-permute-start.5 = (bf16[256,128]{1,0:T(8,128)(2,1)S(1)}, bf16[256,128]{1,0:T(8,128)(2,1)S(1)}, u32[]{:S(2)}, u32[]{:S(2)}) collective-permute-start(bf16[256,128]{1,0:T(8,128)(2,1)S(1)} %constant_dynamic-slice_fusion), channel_id=1, source_target_pairs={{0,24},{8,16},{16,8},{24,0},{1,25},{9,17},{17,9},{25,1},{2,26},{10... | collective-permute-start | bytes 196616 | tf_op jit(solution)/shard_map/ppermute | solution.py:27
  195.0 14.3 %shard_map.174 = (bf16[1024,2048]{1,0:T(8,128)(2,1)}, bf16[1024,2048]{1,0:T(8,128)(2,1)}, bf16[1024,2048]{1,0:T(8,128)(2,1)}, bf16[2048,1024]{1,0:T(8,128)(2,1)}) custom-call(bf16[256,1024]{1,0:T(8,128)(2,1)} %get-tuple-element.26.n0, bf16[256,1024]{1,0:T(8,128)(2,1)} %get-tuple-element.27.n1, bf16[256,1024]{1,0:T(8,128)(2,1)} %bitcast.66, ...), custom_call_target="tpu_custom_call" | custom-call | flops 8589934592 | bytes 16777216 | tf_op jit(solution)/shard_map/pallas_call | solution.py:192
  209.3 44.3 %all-reduce.5.cloned.1.call-done = (f32[256,1024]{1,0:T(8,128)}, f32[256,1024]{1,0:T(8,128)}) async-done(((f32[256,1024]{1,0:T(8,128)}, f32[256,1024]{1,0:T(8,128)}), (f32[256,1024]{1,0:T(8,128)}, f32[256,1024]{1,0:T(8,128)})) %all-reduce.5.cloned.1.call-update) | async-done | bytes 2097168 | tf_op jit(solution)/shard_map/psum | solution.py:211
  253.6 1.8 fusion.18
  255.5 1.6 fusion.17
  257.0 1.3 collective-permute-start.4
  258.3 0.2 add_convert_fusion
  258.5 4.6 %collective-permute-start.1 = (bf16[256,1024]{1,0:T(8,128)(2,1)S(1)}, bf16[256,1024]{1,0:T(8,128)(2,1)S(1)}, u32[]{:S(2)}, u32[]{:S(2)}) collective-permute-start(bf16[256,1024]{1,0:T(8,128)(2,1)S(1)} %add_convert_fusion), channel_id=1, source_target_pairs={{0,8},{8,16},{16,24},{1,9},{9,17},{17,25},{2,10},{10,18},{18,26},{... | collective-permute-start | bytes 1572872 | tf_op jit(solution)/shard_map/ppermute | solution.py:22
  263.1 0.0 collective-permute-done.5
  263.1 0.0 copy-start.9
  263.2 0.6 dynamic-slice_bitcast_fusion.3
  263.7 7.7 %collective-permute-done.4 = bf16[256,1024]{1,0:T(8,128)(2,1)S(1)} collective-permute-done((bf16[256,1024]{1,0:T(8,128)(2,1)S(1)}, bf16[256,1024]{1,0:T(8,128)(2,1)S(1)}, u32[]{:S(2)}, u32[]{:S(2)}) %collective-permute-start.4) | collective-permute-done | bytes 524320 | tf_op jit(solution)/shard_map/ppermute | solution.py:22
  271.4 0.8 fusion.20
  272.3 0.5 collective-permute-done.1
  272.8 0.9 fusion.21
  (33 shorter events, 0.1 us)
Async XLA Ops:
  7.2 44.8 %all-gather.2.cloned.1.call-start = ((), (), s32[]{:S(2)}) async-start(), calls=%async_computation | async-start | bytes 1179648 | tf_op jit(solution)/shard_map/all_gather | solution.py:260
  14.3 10.1 %collective-permute-start.2 = (bf16[768,128]{1,0:T(8,128)(2,1)S(1)}, bf16[768,128]{1,0:T(8,128)(2,1)S(1)}, u32[]{:S(2)}, u32[]{:S(2)}) collective-permute-start(bf16[768,128]{1,0:T(8,128)(2,1)S(1)} %pad_maximum_fusion), channel_id=1, source_target_pairs={{0,24},{8,16},{16,8},{24,0},{1,25},{9,17},{17,9},{25,1},{2,26},{10... | collective-permute-start | bytes 589832 | tf_op jit(solution)/shard_map/ppermute | solution.py:27
  24.4 0.7 copy-start.11
  25.8 111.1 %all-reduce.7.cloned.1.call-start = ((), (), s32[]{:S(2)}) async-start(), calls=%async_computation.2 | async-start | bytes 4194304 | tf_op jit(solution)/shard_map/psum | solution.py:211
  53.8 22.7 %copy-start = (bf16[512,1024]{1,0:T(8,128)(2,1)S(1)}, bf16[512,1024]{1,0:T(8,128)(2,1)}, u32[]{:S(2)}) copy-start(bf16[512,1024]{1,0:T(8,128)(2,1)} %all-gather.2.cloned.1.call-done) | copy-start | bytes 3145732
  53.8 83.1 %copy-start.12 = (f32[1,1024]{1,0:T(1,128)S(1)}, f32[1,1024]{1,0:T(1,128)}, u32[]{:S(2)}) copy-start(f32[1,1024]{1,0:T(1,128)} %gain.7) | copy-start | bytes 12292
  74.9 63.7 %copy-start.3 = (bf16[1,256,1024]{2,1,0:T(8,128)(2,1)S(1)}, bf16[1,256,1024]{2,1,0:T(8,128)(2,1)}, u32[]{:S(2)}) copy-start(bf16[1,256,1024]{2,1,0:T(8,128)(2,1)} %param.11) | copy-start | bytes 1572868
  74.9 63.7 %copy-start.10 = (bf16[1,256,1024]{2,1,0:T(8,128)(2,1)S(1)}, bf16[1,256,1024]{2,1,0:T(8,128)(2,1)}, u32[]{:S(2)}) copy-start(bf16[1,256,1024]{2,1,0:T(8,128)(2,1)} %param.12) | copy-start | bytes 1572868
  75.0 80.5 %copy-start.6 = (bf16[2,256,1024]{2,1,0:T(8,128)(2,1)S(1)}, bf16[2,256,1024]{2,1,0:T(8,128)(2,1)}, u32[]{:S(2)}) copy-start(bf16[2,256,1024]{2,1,0:T(8,128)(2,1)} %param.13) | copy-start | bytes 3145732
  75.0 178.6 %all-reduce.5.cloned.1.call-start = ((), (), s32[]{:S(2)}) async-start(), calls=%async_computation.1 | async-start | bytes 4194304 | tf_op jit(solution)/shard_map/psum | solution.py:211
  141.7 13.7 %collective-permute-start = (bf16[256,1024]{1,0:T(8,128)(2,1)}, bf16[256,1024]{1,0:T(8,128)(2,1)S(1)}, u32[]{:S(2)}, u32[]{:S(2)}) collective-permute-start(bf16[256,1024]{1,0:T(8,128)(2,1)} %get-tuple-element.51), channel_id=1, source_target_pairs={{0,8},{8,16},{16,24},{1,9},{9,17},{17,25},{2,10},{10,18},{18,26},{... | collective-permute-start | bytes 1572872 | tf_op jit(solution)/shard_map/ppermute | solution.py:22
  145.9 22.6 %collective-permute-start.3 = (bf16[256,1024]{1,0:T(8,128)(2,1)}, bf16[256,1024]{1,0:T(8,128)(2,1)S(1)}, u32[]{:S(2)}, u32[]{:S(2)}) collective-permute-start(bf16[256,1024]{1,0:T(8,128)(2,1)} %get-tuple-element.50), channel_id=1, source_target_pairs={{8,0},{16,8},{24,16},{9,1},{17,9},{25,17},{10,2},{18,10},{26,18},{... | collective-permute-start | bytes 1572872 | tf_op jit(solution)/shard_map/ppermute | solution.py:22
  156.3 12.3 %copy-start.5 = (bf16[2,256,1024]{2,1,0:T(8,128)(2,1)S(1)}, bf16[2,256,1024]{2,1,0:T(8,128)(2,1)}, u32[]{:S(2)}) copy-start(bf16[2,256,1024]{2,1,0:T(8,128)(2,1)} %param.14) | copy-start | bytes 3145732
  169.5 21.2 %copy-start.1 = (bf16[256,1024]{1,0:T(8,128)(2,1)S(1)}, bf16[256,1024]{1,0:T(8,128)(2,1)}, u32[]{:S(2)}) copy-start(bf16[256,1024]{1,0:T(8,128)(2,1)} %bitcast_select_fusion.2.rows) | copy-start | bytes 1572868
  190.7 72.4 %collective-permute-start.5 = (bf16[256,128]{1,0:T(8,128)(2,1)S(1)}, bf16[256,128]{1,0:T(8,128)(2,1)S(1)}, u32[]{:S(2)}, u32[]{:S(2)}) collective-permute-start(bf16[256,128]{1,0:T(8,128)(2,1)S(1)} %constant_dynamic-slice_fusion), channel_id=1, source_target_pairs={{0,24},{8,16},{16,8},{24,0},{1,25},{9,17},{17,9},{25,1},{2,26},{10... | collective-permute-start | bytes 196616 | tf_op jit(solution)/shard_map/ppermute | solution.py:27
  195.0 58.6 %copy-start.2 = (bf16[256,1024]{1,0:T(8,128)(2,1)S(1)}, bf16[256,1024]{1,0:T(8,128)(2,1)}, u32[]{:S(2)}) copy-start(bf16[256,1024]{1,0:T(8,128)(2,1)} %get-tuple-element.49.rows) | copy-start | bytes 1572868
  195.0 58.6 %copy-start.13 = (f32[1,1024]{1,0:T(1,128)S(1)}, f32[1,1024]{1,0:T(1,128)}, u32[]{:S(2)}) copy-start(f32[1,1024]{1,0:T(1,128)} %gain.7) | copy-start | bytes 12292
  195.0 60.4 %copy-start.4 = (bf16[256,1024]{1,0:T(8,128)(2,1)S(1)}, bf16[256,1024]{1,0:T(8,128)(2,1)}, u32[]{:S(2)}) copy-start(bf16[256,1024]{1,0:T(8,128)(2,1)} %bitcast_select_fusion.upstream.g1) | copy-start | bytes 1572868
  253.6 4.7 %copy-start.8 = (f32[256,1024]{1,0:T(8,128)S(1)}, f32[256,1024]{1,0:T(8,128)}, u32[]{:S(2)}) copy-start(f32[256,1024]{1,0:T(8,128)} %get-tuple-element.44) | copy-start | bytes 3145732
  253.6 19.2 %copy-start.7 = (bf16[2,256,1024]{2,1,0:T(8,128)(2,1)S(1)}, bf16[2,256,1024]{2,1,0:T(8,128)(2,1)}, u32[]{:S(2)}) copy-start(bf16[2,256,1024]{2,1,0:T(8,128)(2,1)} %param.13) | copy-start | bytes 3145732
  257.0 14.4 %collective-permute-start.4 = (bf16[256,1024]{1,0:T(8,128)(2,1)S(1)}, bf16[256,1024]{1,0:T(8,128)(2,1)S(1)}, u32[]{:S(2)}, u32[]{:S(2)}) collective-permute-start(bf16[256,1024]{1,0:T(8,128)(2,1)S(1)} %fusion.17), channel_id=1, source_target_pairs={{8,0},{16,8},{24,16},{9,1},{17,9},{25,17},{10,2},{18,10},{26,18},{... | collective-permute-start | bytes 1572872 | tf_op jit(solution)/shard_map/ppermute | solution.py:22
  258.5 14.3 %collective-permute-start.1 = (bf16[256,1024]{1,0:T(8,128)(2,1)S(1)}, bf16[256,1024]{1,0:T(8,128)(2,1)S(1)}, u32[]{:S(2)}, u32[]{:S(2)}) collective-permute-start(bf16[256,1024]{1,0:T(8,128)(2,1)S(1)} %add_convert_fusion), channel_id=1, source_target_pairs={{0,8},{8,16},{16,24},{1,9},{9,17},{17,25},{2,10},{10,18},{18,26},{... | collective-permute-start | bytes 1572872 | tf_op jit(solution)/shard_map/ppermute | solution.py:22
  263.1 10.5 %copy-start.9 = (bf16[1,4,256,128]{3,2,1,0:T(8,128)(2,1)}, bf16[1,4,256,128]{3,2,1,0:T(8,128)(2,1)S(1)}, u32[]{:S(2)}) copy-start(bf16[1,4,256,128]{3,2,1,0:T(8,128)(2,1)S(1)} %bitcast_dynamic-update-slice_fusion) | copy-start | bytes 786436
Sparse Core Ops, SparseCore 0:
  25.9 25.9 all-gather.1
  75.1 61.8 all-reduce.6
  190.8 62.7 all-reduce.4

commit v2 on v1

--- a/solution.py
+++ b/solution.py
@@ -16,12 +16,6 @@
 ZEROS = (((0,), (0,)), ((), ()))
 
 
-def passed_along(value, axis, by):
-    count = lax.axis_size(axis)
-    pairs = [(i, i + by) for i in range(count) if 0 <= i + by < count]
-    return lax.ppermute(value, axis, pairs)
-
-
 def mirrored(value, axis):
     count = lax.axis_size(axis)
     return lax.ppermute(value, axis, [(i, count - 1 - i) for i in range(count)])
@@ -48,7 +42,7 @@
     return exponent * (1.0 / jnp.sum(exponent, axis=-1, keepdims=True))
 
 
-def forward_kernel(rows, gain, wq, wk, wv, wo, total, normed):
+def forward_kernel(rows, gain, wq, wk, wv, wo, part, normed, total):
     step = pl.program_id(0)
 
     @pl.when(step == 0)
@@ -65,8 +59,14 @@
         parts.append(low_dot(soft, value_rows[:, head]))
     total[...] += dot(jnp.concatenate(parts, axis=1), wo[...])
 
-
-def backward_kernel(rows, upstream, gain, wq, wk, wv, wo, total, normed, ctx, qg, kg, vg):
+    @pl.when(step == pl.num_programs(0) - 1)
+    def _():
+        part[...] = total[...].astype(part.dtype)
+
+
+def backward_kernel(
+    rows, upstream, gain, wq, wk, wv, wo, part, normed, ctx, qg, kg, vg, total
+):
     step = pl.program_id(0)
 
     @pl.when(step == 0)
@@ -93,6 +93,10 @@
         dot(qg[...], wq[...], ONES) + dot(kg[...], wk[...], ONES) + dot(vg[...], wv[...], ONES)
     )
 
+    @pl.when(step == pl.num_programs(0) - 1)
+    def _():
+        part[...] = total[...].astype(part.dtype)
+
 
 def gradient_kernel(
     n0, n1, g0, g1, c0, c1, q0, q1, k0, k1, v0, v1, wq, wk, wv, wo, turned, upstream
@@ -146,8 +150,11 @@
         grid=(inner // width,),
         in_specs=[whole((count, depth)), whole((1, depth))] + weight_specs(depth, width),
         out_specs=whole((count, depth)),
-        out_shape=jax.ShapeDtypeStruct((count, depth), jnp.float32),
-        scratch_shapes=[pltpu.VMEM((count, depth), jnp.bfloat16)],
+        out_shape=jax.ShapeDtypeStruct((count, depth), jnp.bfloat16),
+        scratch_shapes=[
+            pltpu.VMEM((count, depth), jnp.bfloat16),
+            pltpu.VMEM((count, depth), jnp.float32),
+        ],
         compiler_params=pltpu.CompilerParams(**PARAMS),
         cost_estimate=pl.CostEstimate(
             flops=8 * count * depth * inner + 4 * count * count * inner,
@@ -169,10 +176,11 @@
         + weight_specs(depth, width),
         out_specs=[whole((count, depth)), whole((count, depth))] + [columns(count, width)] * 4,
         out_shape=[
-            jax.ShapeDtypeStruct((count, depth), jnp.float32),
+            jax.ShapeDtypeStruct((count, depth), jnp.bfloat16),
             jax.ShapeDtypeStruct((count, depth), jnp.bfloat16),
         ]
         + [wide] * 4,
+        scratch_shapes=[pltpu.VMEM((count, depth), jnp.float32)],
         compiler_params=pltpu.CompilerParams(**PARAMS),
         cost_estimate=pl.CostEstimate(
             flops=14 * count * depth * inner + 12 * count * count * inner,
@@ -207,19 +215,132 @@
     )(n0, n1, g0, g1, c0, c1, q0, q1, k0, k1, v0, v1)
 
 
-def sent_forward(rows, part):
-    total = lax.psum(part, "head")
-    return passed_along((rows.astype(jnp.float32) + total).astype(jnp.bfloat16), "section", 1)
-
-
-def sent_back(rows, upstream, gain_row, part):
-    normed, unit_rows, inverse = normalize(rows, gain_row)
-    normed_grad = lax.psum(part, "head")
-    gain_full = jnp.sum(normed_grad * unit_rows, axis=0)
-    unit_grad = normed_grad * gain_row
+def relay_kernel(
+    heads, sections, last, x, b, g, gain, fpart, bpart, before,
+    x_next, g_next, gain_out, landed, hop, gains, gains_in, sent, got, hop_sent, hop_got
+):
+    me, section = lax.axis_index("head"), lax.axis_index("section")
+    ahead = lax.rem(section + 1, sections)
+    back = lax.rem(section + sections - 1, sections)
+    share = x.shape[0] // heads
+    peers = [lax.rem(me + d, heads) for d in range(1, heads)]
+
+    barrier = pltpu.get_barrier_semaphore()
+    for peer in peers:
+        pl.semaphore_signal(barrier, inc=1, device_id={"head": peer})
+    for other in (ahead, back):
+        pl.semaphore_signal(barrier, inc=1, device_id={"section": other})
+    pl.semaphore_wait(barrier, heads + 1)
+
+    def rows_of(index):
+        return pl.ds(pl.multiple_of(index * share, share), share)
+
+    def sending(source, target, slot, d, where):
+        return pltpu.make_async_remote_copy(
+            src_ref=source,
+            dst_ref=target,
+            send_sem=sent.at[slot, d],
+            recv_sem=got.at[slot, d],
+            device_id=where,
+            device_id_type=pl.DeviceIdType.MESH,
+        )
+
+    own = rows_of(me)
+    scattered = [
+        [
+            sending(part.at[rows_of(peer)], landed.at[chain, d], chain, d, {"head": peer})
+            for d, peer in enumerate(peers)
+        ]
+        for chain, part in enumerate((fpart, bpart))
+    ]
+    for copies in scattered:
+        for copy in copies:
+            copy.start()
+
+    def summed(chain, part):
+        for copy in scattered[chain]:
+            copy.wait()
+        total = part[own, :].astype(jnp.float32)
+        for d in range(heads - 1):
+            total += landed[chain, d].astype(jnp.float32)
+        return total
+
+    def hopping(chain, target, where):
+        return pltpu.make_async_remote_copy(
+            src_ref=hop.at[chain],
+            dst_ref=target.at[own],
+            send_sem=hop_sent.at[chain],
+            recv_sem=hop_got.at[chain],
+            device_id={"section": where},
+            device_id_type=pl.DeviceIdType.MESH,
+        )
+
+    hop[0] = (x[own, :].astype(jnp.float32) + summed(0, fpart)).astype(hop.dtype)
+    forward_hop = hopping(0, x_next, ahead)
+    forward_hop.start()
+
+    normed_grad = summed(1, bpart)
+    normed, unit_rows, inverse = normalize(b[own, :], gain[...])
+    unit_grad = normed_grad * gain[...]
     along = jnp.mean(unit_grad * unit_rows, axis=-1, keepdims=True)
-    returned = upstream.astype(jnp.float32) + inverse * (unit_grad - unit_rows * along)
-    return passed_along(returned.astype(jnp.bfloat16), "section", -1), gain_full
+    returned = g[own, :].astype(jnp.float32) + inverse * (unit_grad - unit_rows * along)
+    hop[1] = returned.astype(hop.dtype)
+    backward_hop = hopping(1, g_next, back)
+    backward_hop.start()
+
+    products = normed_grad * unit_rows
+    gain_sum = before[...]
+    for start in range(0, share, 8):
+        gain_sum += products[start : start + 8]
+    gathers = []
+    if last:
+        gains[...] = gain_sum
+        for d, peer in enumerate(peers):
+            gathers.append(sending(gains, gains_in.at[d], 4, d, {"head": peer}))
+            gathers[-1].start()
+    for chain, (copy, block) in enumerate(((forward_hop, x_next), (backward_hop, g_next))):
+        copy.wait()
+        for d, peer in enumerate(peers):
+            gathers.append(sending(block.at[own], block.at[own], 2 + chain, d, {"head": peer}))
+            gathers[-1].start()
+    for copy in gathers:
+        copy.wait()
+    if last:
+        for d in range(heads - 1):
+            gain_sum += gains_in[d]
+    gain_out[...] = gain_sum
+
+
+def relay(x, b, g, gain, fpart, bpart, before, last):
+    heads, sections = lax.axis_size("head"), lax.axis_size("section")
+    count, depth = x.shape
+    share = count // heads
+    low = jnp.bfloat16
+    in_vmem = pl.BlockSpec(memory_space=pltpu.VMEM)
+    dma = pltpu.SemaphoreType.DMA
+    return pl.pallas_call(
+        functools.partial(relay_kernel, heads, sections, last),
+        in_specs=[in_vmem] * 7,
+        out_specs=[in_vmem] * 3,
+        out_shape=[
+            jax.ShapeDtypeStruct((count, depth), low),
+            jax.ShapeDtypeStruct((count, depth), low),
+            jax.ShapeDtypeStruct((8, depth), jnp.float32),
+        ],
+        scratch_shapes=[
+            pltpu.VMEM((2, heads - 1, share, depth), low),
+            pltpu.VMEM((2, share, depth), low),
+            pltpu.VMEM((8, depth), jnp.float32),
+            pltpu.VMEM((heads - 1, 8, depth), jnp.float32),
+            dma((5, heads - 1)),
+            dma((5, heads - 1)),
+            dma((2,)),
+            dma((2,)),
+        ],
+        compiler_params=pltpu.CompilerParams(
+            collective_id=int(last), has_side_effects=True, vmem_limit_bytes=24 * 2**20
+        ),
+    )(x, b, g, gain, fpart, bpart, before)
 
 
 def per_device(
@@ -261,25 +382,26 @@
     b0 = restored[:count]
     b1 = jnp.where(own[0] == own[1], x0, restored[count:])
 
-    part = forward_part(x0, weights)
-    x1 = jnp.where(section_index == 0, fresh_tokens[0], sent_forward(x0, part))
-
-    part, *first = backward_part(b0, g0, weights)
-    moved, gain0 = sent_back(b0, g0, norm_gain, part)
-    g1 = jnp.where(section_index == section_count - 1, fresh_cotangents[0], moved)
-
-    part = forward_part(x1, weights)
-    x2 = jnp.where(section_index == 0, fresh_tokens[1], sent_forward(x1, part))
+    first_section = section_index == 0
+    last_section = section_index == section_count - 1
+    forward0 = forward_part(x0, weights)
+    back0, *first = backward_part(b0, g0, weights)
+    nothing = jnp.zeros((8, x0.shape[1]), jnp.float32)
+    made, returned, gain0 = relay(x0, b0, g0, norm_gain, forward0, back0, nothing, False)
+    x1 = jnp.where(first_section, fresh_tokens[0], made)
+    g1 = jnp.where(last_section, fresh_cotangents[0], returned)
+
     arrived1 = mirrored(own_share(x1), "section")
     store = lax.dynamic_update_index_in_dim(store, arrived, held[0], 0)
     store = lax.dynamic_update_index_in_dim(store, arrived1, held[1], 0)
-
-    part, *second = backward_part(b1, g1, weights)
-    moved, gain1 = sent_back(b1, g1, norm_gain, part)
-    g2 = jnp.where(section_index == section_count - 1, fresh_cotangents[1], moved)
+    forward1 = forward_part(x1, weights)
+    back1, *second = backward_part(b1, g1, weights)
+    made, returned, gain1 = relay(x1, b1, g1, norm_gain, forward1, back1, gain0, True)
+    x2 = jnp.where(first_section, fresh_tokens[1], made)
+    g2 = jnp.where(last_section, fresh_cotangents[1], returned)
 
     grads = gradients(first, second, g0, g1)
-    gain = lax.dynamic_slice_in_dim(gain0 + gain1, column_start, share_width, 0)
+    gain = lax.dynamic_slice_in_dim(jnp.sum(gain1, axis=0), column_start, share_width, 0)
     return (x2[None], g2[None], store[None], *(grad[None] for grad in grads), gain[None])
 
 

time: 281 us -> 201 us (0.72)
  waiting for transfers between devices: 140 us -> 17.6 us
  Pallas kernels: 81.1 us -> 143 us
  starting transfers between devices: 20.2 us -> 6.82 us
  other arithmetic: 12 us -> 4.9 us
    psum x2 -> x0, waiting for transfers between devices: 105 us -> none  [sent_forward(): total = lax.psum(part, 'head')]
    pallas_call x0 -> x2, Pallas kernels: none -> 61.2 us  [relay(): pl.pallas_call(functools.partial(relay_kernel, heads, sections, last), in...]
    ppermute x4 -> x0, waiting for transfers between devices: 16.2 us -> none  [passed_along(): return lax.ppermute(value, axis, pairs)]
    ppermute x4 -> x0, starting transfers between devices: 10.7 us -> none  [passed_along(): return lax.ppermute(value, axis, pairs)]
    reduce_sum x4 -> x1, other arithmetic: 6.77 us -> 0.01 us  [per_device(): jnp.sum(gain1, axis=0)]
    unnamed x29 -> x33, local copies, waits for them, and re-layouts: 1.69 us -> 4.53 us
  transfers between devices with their start and end apart: 9 -> 3, of which waited for: 7 -> 2; matrix products, arithmetic and copies ran while one was open for 2% -> 2% of each run, Pallas kernels for 14% -> 40%
where the time goes in v2:
time: 201 us; the launch traced here: 200 us
  Pallas kernels  143 us (71%)
  between operations  19.4 us (10%)
  waiting for transfers between devices  17.6 us (9%)
  local copies, waits for them, and re-layouts  8.05 us (4%)
  starting transfers between devices  6.82 us (3%)
  other arithmetic  4.9 us (2%)
    pallas_call x2, Pallas kernels, relay(): pl.pallas_call(functools.partial(relay_kernel, heads, sections, last), in...  61.2 us
    pallas_call x2, Pallas kernels, backward_part(): pl.pallas_call(backward_kernel, grid=(inner // width,), in_specs=[whole((...  44.1 us
    pallas_call x2, Pallas kernels, forward_part(): pl.pallas_call(forward_kernel, grid=(inner // width,), in_specs=[whole((c...  24.3 us
    pallas_call x1, Pallas kernels, gradients(): pl.pallas_call(gradient_kernel, grid=(inner // width,), in_specs=[whole((...  13.8 us
    all_gather x1, waiting for transfers between devices, per_device(): restored = lax.all_gather(reloads, 'head', axis=1, tiled=True)  12.6 us
    ppermute x2, starting transfers between devices, mirrored(): return lax.ppermute(value, axis, [(i, count - 1 - i) for i in range(count)])  6.79 us
    ppermute x2, waiting for transfers between devices, mirrored(): return lax.ppermute(value, axis, [(i, count - 1 - i) for i in range(count)])  5 us
    unnamed x33, local copies, waits for them, and re-layouts  4.53 us
  transfers between devices with their start and end apart: 3, of which 2 were waited for; matrix products, arithmetic and copies ran while one was open for 2% of the time, Pallas kernels for 40%

profile of v2, /device:TPU:0, one launch (start us, length us, event | category | flops | bytes accessed | tf_op | source)
XLA Modules:
  0.0 200.3 jit_solution(4978380503401301680)
XLA Ops:
  7.2 0.0 all-gather.2.cloned.1.call-start
  7.2 1.0 copy.22
  8.2 0.8 constant_dynamic-slice_fusion.1
  9.0 0.5 fusion.3
  13.4 0.9 dynamic-slice_bitcast_fusion.2
  14.3 5.1 %collective-permute-start = (bf16[768,128]{1,0:T(8,128)(2,1)S(1)}, bf16[768,128]{1,0:T(8,128)(2,1)S(1)}, u32[]{:S(2)}, u32[]{:S(2)}) collective-permute-start(bf16[768,128]{1,0:T(8,128)(2,1)S(1)} %pad_maximum_fusion), channel_id=1, source_target_pairs={{0,24},{8,16},{16,8},{24,0},{1,25},{9,17},{17,9},{25,1},{2,26},{10... | collective-permute-start | bytes 589832 | tf_op jit(solution)/shard_map/ppermute | solution.py:21
  19.4 5.0 %collective-permute-done = bf16[768,128]{1,0:T(8,128)(2,1)S(1)} collective-permute-done((bf16[768,128]{1,0:T(8,128)(2,1)S(1)}, bf16[768,128]{1,0:T(8,128)(2,1)S(1)}, u32[]{:S(2)}, u32[]{:S(2)}) %collective-permute-start) | collective-permute-done | bytes 196640 | tf_op jit(solution)/shard_map/ppermute | solution.py:21
  24.4 0.7 slice.54
  25.1 0.0 all-gather.2.cloned.1.call-update
  26.4 0.0 copy-start.2
  26.4 12.2 %shard_map.170.fpart = bf16[256,1024]{1,0:T(8,128)(2,1)} custom-call(bf16[256,1024]{1,0:T(8,128)(2,1)} %bitcast.44, f32[1,1024]{1,0:T(1,128)} %gain.11, bf16[1024,2048]{1,0:T(8,128)(2,1)} %bitcast.49, bf16[1024,2048]{1,0:T(8,128)(2,1)} %bitcast.53, bf16[1024,2048]{1,0:T(8,128)(2,1)} %bitcast.57, bf16[2048,1024]{1,0:T(8,128)(2,1)} %bitcast.61), custom_call_target="tpu_custom_call" | custom-call | flops 4831838208 | bytes 16777216 | tf_op jit(solution)/shard_map/pallas_call | solution.py:148
  38.7 12.6 %all-gather.2.cloned.1.call-done = bf16[512,1024]{1,0:T(8,128)(2,1)} async-done(((bf16[512,128]{1,0:T(8,128)(2,1)}), bf16[512,1024]{1,0:T(8,128)(2,1)}) %all-gather.2.cloned.1.call-update) | async-done | bytes 1048592 | tf_op jit(solution)/shard_map/all_gather | solution.py:381
  51.3 0.0 copy-done.2
  51.3 2.3 %slice_select_fusion = (bf16[256,1024]{1,0:T(8,128)(2,1)}, bf16[256,1024]{1,0:T(8,128)(2,1)}) fusion(bf16[512,1024]{1,0:T(8,128)(2,1)} %all-gather.2.cloned.1.call-done, pred[]{:T(512)} %bitcast.13, bf16[1,256,1024]{2,1,0:T(8,128)(2,1)S(1)} %copy-done.2), kind=kLoop, calls=%fused_computation | loop fusion | flops 262144 | bytes 2621441 | tf_op jit(solution)/shard_map/jit(_where)/select_n | solution.py:383
  53.5 0.0 copy-start.11
  53.5 0.0 copy-start.13
  53.6 21.8 %shard_map.171 = (bf16[256,1024]{1,0:T(8,128)(2,1)}, bf16[256,1024]{1,0:T(8,128)(2,1)}, bf16[256,2048]{1,0:T(8,128)(2,1)}, bf16[256,2048]{1,0:T(8,128)(2,1)}, bf...) custom-call(bf16[256,1024]{1,0:T(8,128)(2,1)} %get-tuple-element.53.rows.b, bf16[256,1024]{1,0:T(8,128)(2,1)} %bitcast.46, ...), custom_call_target="tpu_custom_call" | custom-call | flops 9126805504 | bytes 16777216 | tf_op jit(solution)/shard_map/pallas_call | solution.py:172
  75.3 0.0 copy-done.5
  75.3 0.0 copy-done.6
  75.4 0.0 copy-done.7
  75.4 0.0 copy-done.11
  75.4 0.0 copy-start.10
  75.4 1.0 copy-done.10
  76.4 29.8 %shard_map.172 = (bf16[256,1024]{1,0:T(8,128)(2,1)S(1)}, bf16[256,1024]{1,0:T(8,128)(2,1)S(1)}, f32[8,1024]{1,0:T(8,128)S(1)}) custom-call(bf16[256,1024]{1,0:T(8,128)(2,1)S(1)} %bitcast.45, bf16[256,1024]{1,0:T(8,128)(2,1)S(1)} %copy-done.5, bf16[256,1024]{1,0:T(8,128)(2,1)S(1)} %bitcast.48, f32[1,1024]{1,0:T(1,128)S(1)} %copy-done.11, ...), custom_call_target="tpu_custom_call" | custom-call | tf_op jit(solution)/shard_map/pallas_call | solution.py:321
  106.3 0.0 copy-done.13
  106.3 0.1 bitcast_select_fusion.2.rows.x
  106.3 0.0 copy-start
  106.4 0.7 copy-done
  107.1 12.1 %shard_map.173.fpart = bf16[256,1024]{1,0:T(8,128)(2,1)} custom-call(bf16[256,1024]{1,0:T(8,128)(2,1)} %copy-done, f32[1,1024]{1,0:T(1,128)} %gain.11, bf16[1024,2048]{1,0:T(8,128)(2,1)} %bitcast.51, bf16[1024,2048]{1,0:T(8,128)(2,1)} %bitcast.55, bf16[1024,2048]{1,0:T(8,128)(2,1)} %bitcast.59, bf16[2048,1024]{1,0:T(8,128)(2,1)} %bitcast.63), custom_call_target="tpu_custom_call" | custom-call | flops 4831838208 | bytes 16777216 | tf_op jit(solution)/shard_map/pallas_call | solution.py:148
  119.3 1.6 collective-permute-start.1
  120.9 0.0 copy-done.14
  120.9 0.9 bitcast_select_fusion.1.upstream.g.g1
  121.8 0.0 copy-start.12
  121.8 22.3 %shard_map.174 = (bf16[256,1024]{1,0:T(8,128)(2,1)}, bf16[256,1024]{1,0:T(8,128)(2,1)}, bf16[256,2048]{1,0:T(8,128)(2,1)}, bf16[256,2048]{1,0:T(8,128)(2,1)}, bf...) custom-call(bf16[256,1024]{1,0:T(8,128)(2,1)} %get-tuple-element.52.rows.b, ...), custom_call_target="tpu_custom_call" | custom-call | flops 9126805504 | bytes 16777216 | tf_op jit(solution)/shard_map/pallas_call | solution.py:172
  144.1 0.0 copy-done.3
  144.1 0.0 copy-done.4
  144.2 0.0 copy-done.8
  144.2 0.0 copy-done.12
  144.2 0.0 copy-start.9
  144.2 1.0 copy-done.9
  145.2 31.3 %shard_map.175 = (bf16[256,1024]{1,0:T(8,128)(2,1)S(1)}, bf16[256,1024]{1,0:T(8,128)(2,1)S(1)}, f32[8,1024]{1,0:T(8,128)S(1)}) custom-call(bf16[256,1024]{1,0:T(8,128)(2,1)S(1)} %copy-done.1, bf16[256,1024]{1,0:T(8,128)(2,1)S(1)} %copy-done.4, bf16[256,1024]{1,0:T(8,128)(2,1)S(1)} %copy-done.3, f32[1,1024]{1,0:T(1,128)S(1)} %copy-done.12, ...), custom_call_target="tpu_custom_call" | custom-call | tf_op jit(solution)/shard_map/pallas_call | solution.py:321
  176.6 0.9 fusion.1
  177.4 0.9 fusion
  178.3 13.8 %shard_map.176 = (bf16[1024,2048]{1,0:T(8,128)(2,1)}, bf16[1024,2048]{1,0:T(8,128)(2,1)}, bf16[1024,2048]{1,0:T(8,128)(2,1)}, bf16[2048,1024]{1,0:T(8,128)(2,1)}) custom-call(bf16[256,1024]{1,0:T(8,128)(2,1)} %get-tuple-element.37.n0, bf16[256,1024]{1,0:T(8,128)(2,1)} %get-tuple-element.38.n1, bf16[256,1024]{1,0:T(8,128)(2,1)} %bitcast.47, ...), custom_call_target="tpu_custom_call" | custom-call | flops 8589934592 | bytes 16777216 | tf_op jit(solution)/shard_map/pallas_call | solution.py:200
  192.1 0.6 dynamic-slice_bitcast_fusion.3
  192.7 0.0 collective-permute-done.1
  192.7 0.0 copy-start.15
  192.7 0.7 copy-done.15
  (16 shorter events, 0.1 us)
Async XLA Ops:
  7.2 44.1 %all-gather.2.cloned.1.call-start = ((), (), s32[]{:S(2)}) async-start(), calls=%async_computation | async-start | bytes 1179648 | tf_op jit(solution)/shard_map/all_gather | solution.py:381
  14.3 10.1 %collective-permute-start = (bf16[768,128]{1,0:T(8,128)(2,1)S(1)}, bf16[768,128]{1,0:T(8,128)(2,1)S(1)}, u32[]{:S(2)}, u32[]{:S(2)}) collective-permute-start(bf16[768,128]{1,0:T(8,128)(2,1)S(1)} %pad_maximum_fusion), channel_id=1, source_target_pairs={{0,24},{8,16},{16,8},{24,0},{1,25},{9,17},{17,9},{25,1},{2,26},{10... | collective-permute-start | bytes 589832 | tf_op jit(solution)/shard_map/ppermute | solution.py:21
  26.4 24.8 %copy-start.2 = (bf16[1,256,1024]{2,1,0:T(8,128)(2,1)S(1)}, bf16[1,256,1024]{2,1,0:T(8,128)(2,1)}, u32[]{:S(2)}) copy-start(bf16[1,256,1024]{2,1,0:T(8,128)(2,1)} %param.11) | copy-start | bytes 1572868
  53.5 21.8 %copy-start.5 = (bf16[256,1024]{1,0:T(8,128)(2,1)S(1)}, bf16[256,1024]{1,0:T(8,128)(2,1)}, u32[]{:S(2)}) copy-start(bf16[256,1024]{1,0:T(8,128)(2,1)} %get-tuple-element.53.rows.b) | copy-start | bytes 1572868
  53.5 21.8 %copy-start.6 = (bf16[1,256,1024]{2,1,0:T(8,128)(2,1)S(1)}, bf16[1,256,1024]{2,1,0:T(8,128)(2,1)}, u32[]{:S(2)}) copy-start(bf16[1,256,1024]{2,1,0:T(8,128)(2,1)} %param.12) | copy-start | bytes 1572868
  53.5 21.8 %copy-start.7 = (bf16[256,1024]{1,0:T(8,128)(2,1)S(1)}, bf16[256,1024]{1,0:T(8,128)(2,1)}, u32[]{:S(2)}) copy-start(bf16[256,1024]{1,0:T(8,128)(2,1)} %shard_map.170.fpart) | copy-start | bytes 1572868
  53.5 21.8 %copy-start.11 = (f32[1,1024]{1,0:T(1,128)S(1)}, f32[1,1024]{1,0:T(1,128)}, u32[]{:S(2)}) copy-start(f32[1,1024]{1,0:T(1,128)} %gain.11) | copy-start | bytes 12292
  53.5 52.7 %copy-start.13 = (bf16[2,256,1024]{2,1,0:T(8,128)(2,1)S(1)}, bf16[2,256,1024]{2,1,0:T(8,128)(2,1)}, u32[]{:S(2)}) copy-start(bf16[2,256,1024]{2,1,0:T(8,128)(2,1)} %param.13) | copy-start | bytes 3145732
  75.4 1.0 copy-start.10
  106.3 0.8 copy-start
  107.1 13.8 %copy-start.14 = (bf16[2,256,1024]{2,1,0:T(8,128)(2,1)S(1)}, bf16[2,256,1024]{2,1,0:T(8,128)(2,1)}, u32[]{:S(2)}) copy-start(bf16[2,256,1024]{2,1,0:T(8,128)(2,1)} %param.14) | copy-start | bytes 3145732
  119.3 73.4 %collective-permute-start.1 = (bf16[256,128]{1,0:T(8,128)(2,1)S(1)}, bf16[256,128]{1,0:T(8,128)(2,1)S(1)}, u32[]{:S(2)}, u32[]{:S(2)}) collective-permute-start(bf16[256,128]{1,0:T(8,128)(2,1)S(1)} %constant_dynamic-slice_fusion), channel_id=1, source_target_pairs={{0,24},{8,16},{16,8},{24,0},{1,25},{9,17},{17,9},{25,1},{2,26},{10... | collective-permute-start | bytes 196616 | tf_op jit(solution)/shard_map/ppermute | solution.py:21
  121.8 22.3 %copy-start.1 = (bf16[256,1024]{1,0:T(8,128)(2,1)S(1)}, bf16[256,1024]{1,0:T(8,128)(2,1)}, u32[]{:S(2)}) copy-start(bf16[256,1024]{1,0:T(8,128)(2,1)} %copy-done) | copy-start | bytes 1572868
  121.8 22.3 %copy-start.3 = (bf16[256,1024]{1,0:T(8,128)(2,1)S(1)}, bf16[256,1024]{1,0:T(8,128)(2,1)}, u32[]{:S(2)}) copy-start(bf16[256,1024]{1,0:T(8,128)(2,1)} %bitcast_select_fusion.1.upstream.g.g1) | copy-start | bytes 1572868
  121.8 22.4 %copy-start.4 = (bf16[256,1024]{1,0:T(8,128)(2,1)S(1)}, bf16[256,1024]{1,0:T(8,128)(2,1)}, u32[]{:S(2)}) copy-start(bf16[256,1024]{1,0:T(8,128)(2,1)} %get-tuple-element.52.rows.b) | copy-start | bytes 1572868
  121.8 22.4 %copy-start.8 = (bf16[256,1024]{1,0:T(8,128)(2,1)S(1)}, bf16[256,1024]{1,0:T(8,128)(2,1)}, u32[]{:S(2)}) copy-start(bf16[256,1024]{1,0:T(8,128)(2,1)} %shard_map.173.fpart) | copy-start | bytes 1572868
  121.8 22.4 %copy-start.12 = (f32[1,1024]{1,0:T(1,128)S(1)}, f32[1,1024]{1,0:T(1,128)}, u32[]{:S(2)}) copy-start(f32[1,1024]{1,0:T(1,128)} %gain.11) | copy-start | bytes 12292
  144.2 1.0 copy-start.9
  192.7 0.7 copy-start.15
Sparse Core Ops, SparseCore 0:
  25.3 25.9 all-gather.1

commit v3 on v2

--- a/solution.py
+++ b/solution.py
@@ -378,13 +378,14 @@
 
     travel = mirrored(jnp.concatenate([own_share(x0), held0, held1], axis=0), "section")
     arrived, reloads = travel[:count], travel[count:]
-    restored = lax.all_gather(reloads, "head", axis=1, tiled=True)
-    b0 = restored[:count]
-    b1 = jnp.where(own[0] == own[1], x0, restored[count:])
+    b0 = lax.all_gather(reloads[:count], "head", axis=1, tiled=True)
 
     first_section = section_index == 0
     last_section = section_index == section_count - 1
     forward0 = forward_part(x0, weights)
+    later, forward0 = lax.optimization_barrier((reloads[count:], forward0))
+    restored = lax.all_gather(later, "head", axis=1, tiled=True)
+    b1 = jnp.where(own[0] == own[1], x0, restored)
     back0, *first = backward_part(b0, g0, weights)
     nothing = jnp.zeros((8, x0.shape[1]), jnp.float32)
     made, returned, gain0 = relay(x0, b0, g0, norm_gain, forward0, back0, nothing, False)

time: 201 us -> 187 us (0.930)
  blocking collectives: 0 us -> 20.9 us
  waiting for transfers between devices: 17.6 us -> 0.01 us
  between operations: 19.4 us -> 6.05 us
  Pallas kernels: 143 us -> 140 us
    all_gather x0 -> x2, blocking collectives: none -> 20.9 us  [the longest x1 11.1 us: per_device(): b0 = lax.all_gather(reloads[:count], 'head', axis=1, tiled=True)]
    all_gather x1 -> x0, waiting for transfers between devices: 12.6 us -> none  [per_device(): restored = lax.all_gather(reloads, 'head', axis=1, tiled=True)]
    ppermute x2, waiting for transfers between devices: 5 us -> 0.01 us  [mirrored(): return lax.ppermute(value, axis, [(i, count - 1 - i) for i in range(count)])]
    pallas_call x2, Pallas kernels: 61.2 us -> 58.8 us  [relay(): pl.pallas_call(functools.partial(relay_kernel, heads, sections, last), in...]
  transfers between devices with their start and end apart: 3 -> 2, of which waited for: 2 -> 0; matrix products, arithmetic and copies ran while one was open for 2% -> 2% of each run, Pallas kernels for 40% -> 42%
where the time goes in v3:
time: 187 us; the launch traced here: 186 us
  Pallas kernels  140 us (75%)
  blocking collectives  20.9 us (11%)
  starting transfers between devices  7.49 us (4%)
  local copies, waits for them, and re-layouts  7.4 us (4%)
  between operations  6.05 us (3%)
  other arithmetic  3.49 us (2%)
    pallas_call x2, Pallas kernels, relay(): pl.pallas_call(functools.partial(relay_kernel, heads, sections, last), in...  58.8 us
    pallas_call x2, Pallas kernels, backward_part(): pl.pallas_call(backward_kernel, grid=(inner // width,), in_specs=[whole((...  43.6 us
    pallas_call x2, Pallas kernels, forward_part(): pl.pallas_call(forward_kernel, grid=(inner // width,), in_specs=[whole((c...  24.2 us
    pallas_call x1, Pallas kernels, gradients(): pl.pallas_call(gradient_kernel, grid=(inner // width,), in_specs=[whole((...  13.8 us
    all_gather x1, blocking collectives, per_device(): b0 = lax.all_gather(reloads[:count], 'head', axis=1, tiled=True)  11.1 us
    all_gather x1, blocking collectives, per_device(): restored = lax.all_gather(later, 'head', axis=1, tiled=True)  9.82 us
    ppermute x2, starting transfers between devices, mirrored(): return lax.ppermute(value, axis, [(i, count - 1 - i) for i in range(count)])  7.49 us
    unnamed x33, local copies, waits for them, and re-layouts  4.52 us
  transfers between devices with their start and end apart: 2, of which 0 were waited for; matrix products, arithmetic and copies ran while one was open for 2% of the time, Pallas kernels for 42%

profile of v3, /device:TPU:0, one launch (start us, length us, event | category | flops | bytes accessed | tf_op | source)
XLA Modules:
  0.0 185.7 jit_solution(10302041494823909232)
XLA Ops:
  0.6 1.0 copy.22
  1.6 0.8 constant_dynamic-slice_fusion.1
  2.4 0.5 fusion.4
  6.8 0.9 dynamic-slice_bitcast_fusion.2
  7.7 5.1 %collective-permute-start = (bf16[768,128]{1,0:T(8,128)(2,1)S(1)}, bf16[768,128]{1,0:T(8,128)(2,1)S(1)}, u32[]{:S(2)}, u32[]{:S(2)}) collective-permute-start(bf16[768,128]{1,0:T(8,128)(2,1)S(1)} %pad_maximum_fusion), channel_id=1, source_target_pairs={{0,24},{8,16},{16,8},{24,0},{1,25},{9,17},{17,9},{25,1},{2,26},{10... | collective-permute-start | bytes 589832 | tf_op jit(solution)/shard_map/ppermute | solution.py:21
  12.9 12.0 %shard_map.170.fpart = bf16[256,1024]{1,0:T(8,128)(2,1)} custom-call(bf16[256,1024]{1,0:T(8,128)(2,1)} %bitcast.44, f32[1,1024]{1,0:T(1,128)} %gain.11, bf16[1024,2048]{1,0:T(8,128)(2,1)} %bitcast.49, bf16[1024,2048]{1,0:T(8,128)(2,1)} %bitcast.53, bf16[1024,2048]{1,0:T(8,128)(2,1)} %bitcast.57, bf16[2048,1024]{1,0:T(8,128)(2,1)} %bitcast.61), custom_call_target="tpu_custom_call" | custom-call | flops 4831838208 | bytes 16777216 | tf_op jit(solution)/shard_map/pallas_call | solution.py:148
  26.2 0.0 collective-permute-done
  26.2 11.1 %all_gather.6.rows.b = bf16[256,1024]{1,0:T(8,128)(2,1)} all-gather(bf16[256,128]{1,0:T(8,128)(2,1)S(1)} %get-tuple-element.59), channel_id=1, replica_groups=mesh['section'=4,'head'=8] {'head'}, dimensions={1}, use_global_device_ids=true | all-gather | bytes 589824 | tf_op jit(solution)/shard_map/all_gather | solution.py:381
  37.3 0.0 copy-start
  37.3 0.0 copy-start.5
  37.3 0.0 copy-start.6
  37.3 0.0 copy-start.13
  37.3 21.8 %shard_map.171 = (bf16[256,1024]{1,0:T(8,128)(2,1)}, bf16[256,1024]{1,0:T(8,128)(2,1)}, bf16[256,2048]{1,0:T(8,128)(2,1)}, bf16[256,2048]{1,0:T(8,128)(2,1)}, bf...) custom-call(bf16[256,1024]{1,0:T(8,128)(2,1)} %all_gather.6.rows.b, bf16[256,1024]{1,0:T(8,128)(2,1)} %bitcast.46, ...), custom_call_target="tpu_custom_call" | custom-call | flops 9126805504 | bytes 16777216 | tf_op jit(solution)/shard_map/pallas_call | solution.py:172
  59.1 0.0 copy-done
  59.1 0.0 copy-done.5
  59.1 0.0 copy-done.6
  59.1 0.0 copy-done.7
  59.1 0.0 copy-done.11
  59.2 0.0 copy-start.10
  59.2 1.0 copy-done.10
  60.2 28.1 %shard_map.172 = (bf16[256,1024]{1,0:T(8,128)(2,1)S(1)}, bf16[256,1024]{1,0:T(8,128)(2,1)S(1)}, f32[8,1024]{1,0:T(8,128)S(1)}) custom-call(bf16[256,1024]{1,0:T(8,128)(2,1)S(1)} %bitcast.45, bf16[256,1024]{1,0:T(8,128)(2,1)S(1)} %copy-done.5, bf16[256,1024]{1,0:T(8,128)(2,1)S(1)} %bitcast.48, f32[1,1024]{1,0:T(1,128)S(1)} %copy-done.11, ...), custom_call_target="tpu_custom_call" | custom-call | tf_op jit(solution)/shard_map/pallas_call | solution.py:321
  88.3 0.0 copy-done.13
  88.3 0.1 bitcast_select_fusion.2.rows.x
  88.4 0.0 copy-start.1
  88.4 0.7 copy-done.1
  89.2 12.1 %shard_map.173.fpart = bf16[256,1024]{1,0:T(8,128)(2,1)} custom-call(bf16[256,1024]{1,0:T(8,128)(2,1)} %copy-done.1, f32[1,1024]{1,0:T(1,128)} %gain.11, bf16[1024,2048]{1,0:T(8,128)(2,1)} %bitcast.51, bf16[1024,2048]{1,0:T(8,128)(2,1)} %bitcast.55, bf16[1024,2048]{1,0:T(8,128)(2,1)} %bitcast.59, bf16[2048,1024]{1,0:T(8,128)(2,1)} %bitcast.63), custom_call_target="tpu_custom_call" | custom-call | flops 4831838208 | bytes 16777216 | tf_op jit(solution)/shard_map/pallas_call | solution.py:148
  101.3 9.8 %all_gather.7 = bf16[256,1024]{1,0:T(8,128)(2,1)S(1)} all-gather(bf16[256,128]{1,0:T(8,128)(2,1)S(1)} %get-tuple-element.35), channel_id=1, replica_groups=mesh['section'=4,'head'=8] {'head'}, dimensions={1}, use_global_device_ids=true | all-gather | bytes 589824 | tf_op jit(solution)/shard_map/all_gather | solution.py:387
  111.1 2.3 %collective-permute-start.1 = (bf16[256,128]{1,0:T(8,128)(2,1)S(1)}, bf16[256,128]{1,0:T(8,128)(2,1)S(1)}, u32[]{:S(2)}, u32[]{:S(2)}) collective-permute-start(bf16[256,128]{1,0:T(8,128)(2,1)S(1)} %constant_dynamic-slice_fusion), channel_id=1, source_target_pairs={{0,24},{8,16},{16,8},{24,0},{1,25},{9,17},{17,9},{25,1},{2,26},{10... | collective-permute-start | bytes 196616 | tf_op jit(solution)/shard_map/ppermute | solution.py:21
  113.5 0.8 broadcast_select_fusion.rows.b
  114.3 0.0 copy-done.14
  114.3 0.9 bitcast_select_fusion.1.upstream.g.g1
  115.2 0.0 copy-start.12
  115.2 21.8 %shard_map.174 = (bf16[256,1024]{1,0:T(8,128)(2,1)}, bf16[256,1024]{1,0:T(8,128)(2,1)}, bf16[256,2048]{1,0:T(8,128)(2,1)}, bf16[256,2048]{1,0:T(8,128)(2,1)}, bf...) custom-call(bf16[256,1024]{1,0:T(8,128)(2,1)} %broadcast_select_fusion.rows.b, ...), custom_call_target="tpu_custom_call" | custom-call | flops 9126805504 | bytes 16777216 | tf_op jit(solution)/shard_map/pallas_call | solution.py:172
  137.0 0.0 copy-done.2
  137.0 0.0 copy-done.3
  137.0 0.0 copy-done.4
  137.0 0.0 copy-done.8
  137.1 0.0 copy-done.12
  137.1 0.0 copy-start.9
  137.1 1.0 copy-done.9
  138.1 30.7 %shard_map.175 = (bf16[256,1024]{1,0:T(8,128)(2,1)S(1)}, bf16[256,1024]{1,0:T(8,128)(2,1)S(1)}, f32[8,1024]{1,0:T(8,128)S(1)}) custom-call(bf16[256,1024]{1,0:T(8,128)(2,1)S(1)} %copy-done.2, bf16[256,1024]{1,0:T(8,128)(2,1)S(1)} %copy-done.4, bf16[256,1024]{1,0:T(8,128)(2,1)S(1)} %copy-done.3, f32[1,1024]{1,0:T(1,128)S(1)} %copy-done.12, ...), custom_call_target="tpu_custom_call" | custom-call | tf_op jit(solution)/shard_map/pallas_call | solution.py:321
  168.8 0.9 fusion.1
  169.7 0.9 fusion
  170.5 13.8 %shard_map.176 = (bf16[1024,2048]{1,0:T(8,128)(2,1)}, bf16[1024,2048]{1,0:T(8,128)(2,1)}, bf16[1024,2048]{1,0:T(8,128)(2,1)}, bf16[2048,1024]{1,0:T(8,128)(2,1)}) custom-call(bf16[256,1024]{1,0:T(8,128)(2,1)} %get-tuple-element.41.n0, bf16[256,1024]{1,0:T(8,128)(2,1)} %get-tuple-element.42.n1, bf16[256,1024]{1,0:T(8,128)(2,1)} %bitcast.47, ...), custom_call_target="tpu_custom_call" | custom-call | flops 8589934592 | bytes 16777216 | tf_op jit(solution)/shard_map/pallas_call | solution.py:200
  184.4 0.6 dynamic-slice_bitcast_fusion.3
  185.0 0.0 collective-permute-done.1
  185.0 0.0 copy-start.15
  185.0 0.7 copy-done.15
  (15 shorter events, 0.1 us)
Async XLA Ops:
  7.7 18.5 %collective-permute-start = (bf16[768,128]{1,0:T(8,128)(2,1)S(1)}, bf16[768,128]{1,0:T(8,128)(2,1)S(1)}, u32[]{:S(2)}, u32[]{:S(2)}) collective-permute-start(bf16[768,128]{1,0:T(8,128)(2,1)S(1)} %pad_maximum_fusion), channel_id=1, source_target_pairs={{0,24},{8,16},{16,8},{24,0},{1,25},{9,17},{17,9},{25,1},{2,26},{10... | collective-permute-start | bytes 589832 | tf_op jit(solution)/shard_map/ppermute | solution.py:21
  37.3 21.8 %copy-start = (bf16[1,256,1024]{2,1,0:T(8,128)(2,1)S(1)}, bf16[1,256,1024]{2,1,0:T(8,128)(2,1)}, u32[]{:S(2)}) copy-start(bf16[1,256,1024]{2,1,0:T(8,128)(2,1)} %param.11) | copy-start | bytes 1572868
  37.3 21.8 %copy-start.5 = (bf16[256,1024]{1,0:T(8,128)(2,1)S(1)}, bf16[256,1024]{1,0:T(8,128)(2,1)}, u32[]{:S(2)}) copy-start(bf16[256,1024]{1,0:T(8,128)(2,1)} %all_gather.6.rows.b) | copy-start | bytes 1572868
  37.3 21.8 %copy-start.6 = (bf16[1,256,1024]{2,1,0:T(8,128)(2,1)S(1)}, bf16[1,256,1024]{2,1,0:T(8,128)(2,1)}, u32[]{:S(2)}) copy-start(bf16[1,256,1024]{2,1,0:T(8,128)(2,1)} %param.12) | copy-start | bytes 1572868
  37.3 21.8 %copy-start.7 = (bf16[256,1024]{1,0:T(8,128)(2,1)S(1)}, bf16[256,1024]{1,0:T(8,128)(2,1)}, u32[]{:S(2)}) copy-start(bf16[256,1024]{1,0:T(8,128)(2,1)} %shard_map.170.fpart) | copy-start | bytes 1572868
  37.3 21.8 %copy-start.11 = (f32[1,1024]{1,0:T(1,128)S(1)}, f32[1,1024]{1,0:T(1,128)}, u32[]{:S(2)}) copy-start(f32[1,1024]{1,0:T(1,128)} %gain.11) | copy-start | bytes 12292
  37.3 51.0 %copy-start.13 = (bf16[2,256,1024]{2,1,0:T(8,128)(2,1)S(1)}, bf16[2,256,1024]{2,1,0:T(8,128)(2,1)}, u32[]{:S(2)}) copy-start(bf16[2,256,1024]{2,1,0:T(8,128)(2,1)} %param.13) | copy-start | bytes 3145732
  59.2 1.0 copy-start.10
  88.4 0.8 copy-start.1
  89.2 25.2 %copy-start.14 = (bf16[2,256,1024]{2,1,0:T(8,128)(2,1)S(1)}, bf16[2,256,1024]{2,1,0:T(8,128)(2,1)}, u32[]{:S(2)}) copy-start(bf16[2,256,1024]{2,1,0:T(8,128)(2,1)} %param.14) | copy-start | bytes 3145732
  111.1 73.8 %collective-permute-start.1 = (bf16[256,128]{1,0:T(8,128)(2,1)S(1)}, bf16[256,128]{1,0:T(8,128)(2,1)S(1)}, u32[]{:S(2)}, u32[]{:S(2)}) collective-permute-start(bf16[256,128]{1,0:T(8,128)(2,1)S(1)} %constant_dynamic-slice_fusion), channel_id=1, source_target_pairs={{0,24},{8,16},{16,8},{24,0},{1,25},{9,17},{17,9},{25,1},{2,26},{10... | collective-permute-start | bytes 196616 | tf_op jit(solution)/shard_map/ppermute | solution.py:21
  115.2 21.8 %copy-start.2 = (bf16[256,1024]{1,0:T(8,128)(2,1)S(1)}, bf16[256,1024]{1,0:T(8,128)(2,1)}, u32[]{:S(2)}) copy-start(bf16[256,1024]{1,0:T(8,128)(2,1)} %copy-done.1) | copy-start | bytes 1572868
  115.2 21.8 %copy-start.3 = (bf16[256,1024]{1,0:T(8,128)(2,1)S(1)}, bf16[256,1024]{1,0:T(8,128)(2,1)}, u32[]{:S(2)}) copy-start(bf16[256,1024]{1,0:T(8,128)(2,1)} %bitcast_select_fusion.1.upstream.g.g1) | copy-start | bytes 1572868
  115.2 21.8 %copy-start.4 = (bf16[256,1024]{1,0:T(8,128)(2,1)S(1)}, bf16[256,1024]{1,0:T(8,128)(2,1)}, u32[]{:S(2)}) copy-start(bf16[256,1024]{1,0:T(8,128)(2,1)} %broadcast_select_fusion.rows.b) | copy-start | bytes 1572868
  115.2 21.9 %copy-start.8 = (bf16[256,1024]{1,0:T(8,128)(2,1)S(1)}, bf16[256,1024]{1,0:T(8,128)(2,1)}, u32[]{:S(2)}) copy-start(bf16[256,1024]{1,0:T(8,128)(2,1)} %shard_map.173.fpart) | copy-start | bytes 1572868
  115.2 21.9 %copy-start.12 = (f32[1,1024]{1,0:T(1,128)S(1)}, f32[1,1024]{1,0:T(1,128)}, u32[]{:S(2)}) copy-start(f32[1,1024]{1,0:T(1,128)} %gain.11) | copy-start | bytes 12292
  137.1 1.0 copy-start.9
  185.0 0.7 copy-start.15
